TPU v7x, 32 devices: a whole 2x2x4 slice. The times are simulated.
32 devices in a mesh: seq: 8 (over y, x, core), head: 4 (over z).
Axes of the slice: x: 2, y: 2, z: 4, core: 2. Of those that a mesh axis runs over, the one named last changes fastest.
Arguments:
- hidden: bfloat16 [2, 2048, 768], P(None, 'seq'), may hold values from -6 to 6
- cotangent: bfloat16 [2, 2048, 768], P(None, 'seq'), may hold values from -6 to 6
- norm_gain: float32 [2, 768], replicated, may hold values from 0.5 to 1.5
- w_in_zx: bfloat16 [2, 768, 2, 1536], P(None, None, None, 'head'), may hold values from -0.21875 to 0.21875
- w_in_dt: bfloat16 [2, 768, 24], P(None, None, 'head'), may hold values from -0.21875 to 0.21875
- w_in_bc: bfloat16 [2, 768, 256], replicated, may hold values from -0.21875 to 0.21875
- conv_x: float32 [2, 4, 1536], P(None, None, 'head'), may hold values from -3 to 3
- conv_x_bias: float32 [2, 1536], P(None, 'head'), may hold values from -3 to 3
- conv_bc: float32 [2, 4, 256], replicated, may hold values from -3 to 3
- conv_bc_bias: float32 [2, 256], replicated, may hold values from -3 to 3
- dt_bias: float32 [2, 24], P(None, 'head'), may hold values from -10 to -4
- a_log: float32 [2, 24], P(None, 'head'), may hold values from 0 to 2.77
- d_skip: float32 [2, 24], P(None, 'head'), may hold values from 0.5 to 1.5
- gate_norm: float32 [2, 1536], P(None, 'head'), may hold values from 0.5 to 1.5
- w_out: bfloat16 [2, 1536, 768], P(None, 'head'), may hold values from -0.15625 to 0.15625
Outputs:
- final_out: float32 [2, 2048, 768], P(None, 'seq')
- hidden_grad: float32 [2, 2048, 768], P(None, 'seq')
- norm_gain_grad: float32 [2, 768], replicated
- w_in_zx_grad: float32 [2, 768, 2, 1536], P(None, None, None, 'head')
- w_in_dt_grad: float32 [2, 768, 24], P(None, None, 'head')
- w_in_bc_grad: float32 [2, 768, 256], replicated
- conv_x_grad: float32 [2, 4, 1536], P(None, None, 'head')
- conv_x_bias_grad: float32 [2, 1536], P(None, 'head')
- conv_bc_grad: float32 [2, 4, 256], replicated
- conv_bc_bias_grad: float32 [2, 256], replicated
- dt_bias_grad: float32 [2, 24], P(None, 'head')
- a_log_grad: float32 [2, 24], P(None, 'head')
- d_skip_grad: float32 [2, 24], P(None, 'head')
- gate_norm_grad: float32 [2, 1536], P(None, 'head')
- w_out_grad: float32 [2, 1536, 768], P(None, 'head')
All inputs are finite; a program needn't handle non-finite values.
Results may differ from a plain program's by a relative error of at most 0.015.
Values may be sent and summed in bfloat16 or wider, within the bound.
No kernel may reach another device: no remote copies, remote signals or barrier semaphores. Data moves between devices by JAX's collectives and lax.ppermute only.
A program may use at most 128 MiB of HBM per device.

v0:
```python
import jax
import jax.numpy as jnp
from jax import lax
from jax.sharding import PartitionSpec as P

EPSILON = 1e-05
PRECISE = lax.Precision.HIGHEST


def shifted(shard, axis, by):
    peers = lax.axis_size(axis)
    pairs = [(i, i + by) for i in range(peers) if 0 <= i + by < peers]
    return lax.ppermute(shard, axis, pairs)


def entering(part, axis, combine, identity, reverse):
    count = lax.axis_size(axis)
    place = lax.axis_index(axis)
    ahead = count - 1 - place if reverse else place
    gathered = jax.tree.map(lambda a: lax.all_gather(a, axis), part)
    state = jax.tree.map(lambda a, e: jnp.zeros_like(a) + jnp.asarray(e, a.dtype), part, identity)

    def one(lap, state):
        source = count - 1 - lap if reverse else lap
        return combine(
            state, jax.tree.map(lambda a: lax.dynamic_index_in_dim(a, source, 0, False), gathered)
        )

    return lax.fori_loop(0, ahead, one, state)


def for_sending(shard):
    return jax.tree.map(lambda a: a.astype(jnp.bfloat16) if a.dtype == jnp.float32 else a, shard)


def span_step(state_in, inputs, step_size, log_decay, b_rows, c_rows, forward_only):
    length = inputs.shape[1]
    cumulative = jnp.cumsum(log_decay, axis=1)
    places = jnp.arange(length)
    causal = (places[:, None] >= places[None, :])[None, :, :, None]
    spread = cumulative[:, :, None, :] - cumulative[:, None, :, :]
    decays = jnp.where(causal, jnp.exp(jnp.where(causal, spread, 0.0)), 0.0)
    if forward_only:
        scores = jnp.einsum(
            "btn,bsn->bts",
            c_rows.astype(jnp.bfloat16),
            b_rows.astype(jnp.bfloat16),
            preferred_element_type=jnp.float32,
        )
    else:
        scores = jnp.einsum("btn,bsn->bts", c_rows, b_rows, precision=PRECISE)
    mixing = scores[..., None] * decays * step_size[:, None, :, :]
    outputs = jnp.einsum("btsh,bshp->bthp", mixing, inputs, precision=PRECISE)
    outputs = outputs + jnp.exp(cumulative)[..., None] * jnp.einsum(
        "btn,bhpn->bthp", c_rows, state_in, precision=PRECISE
    )
    final_sum = cumulative[:, -1]
    weights_tail = jnp.exp(final_sum[:, None, :] - cumulative) * step_size
    state_out = jnp.exp(final_sum)[:, :, None, None] * state_in + jnp.einsum(
        "bsh,bshp,bsn->bhpn", weights_tail, inputs, b_rows, precision=PRECISE
    )
    return (state_out, outputs)


def ssd_parts(inputs, step_size, log_decay, b_rows, c_rows, forward_only):
    batch_count, length, head_count, head_size = inputs.shape
    state_now = jnp.zeros((batch_count, head_count, head_size, b_rows.shape[-1]), jnp.float32)
    state_now, block_out = span_step(
        state_now, inputs, step_size, log_decay, b_rows, c_rows, forward_only
    )
    pieces = [block_out]
    return (jnp.concatenate(pieces, 1), state_now)


def ssd_device(inputs, steps_raw, bias_dt, log_rate, skip_gain, b_rows, c_rows, state_in):
    step_size = jax.nn.softplus(steps_raw + bias_dt)
    log_decay = -jnp.exp(log_rate) * step_size
    local_out, state_local = ssd_parts(inputs, step_size, log_decay, b_rows, c_rows, False)
    cumulative = jnp.cumsum(log_decay, axis=1)
    carried = jnp.exp(cumulative)[..., None] * jnp.einsum(
        "btn,bhpn->bthp", c_rows, state_in, precision=PRECISE
    )
    outputs = local_out + carried + skip_gain[:, None] * inputs
    state_out = jnp.exp(cumulative[:, -1])[:, :, None, None] * state_in + state_local
    return (outputs, state_out)


def chain_combine(earlier, later):
    return (earlier[0] * later[0], later[0][..., None, None] * earlier[1] + later[1])


def back_combine(earlier, later):
    return (earlier[0] * later[0], later[1] + later[0][..., None, None] * earlier[1])


def rms_scale(values, gain):
    return values * lax.rsqrt(jnp.mean(values * values, -1, keepdims=True) + EPSILON) * gain


def causal_apply(padded, kernel, offset, length):
    result = kernel[0] * padded[:, 0:length].astype(jnp.float32)
    for tap_index in range(1, kernel.shape[0]):
        result = result + kernel[tap_index] * padded[:, tap_index : tap_index + length].astype(
            jnp.float32
        )
    return result + offset


def gather_stream(stream_part):
    return lax.all_gather(stream_part, "head", axis=0, tiled=True)


def shards(
    hidden,
    cotangent,
    norm_gain,
    w_in_zx,
    w_in_dt,
    w_in_bc,
    conv_x,
    conv_x_bias,
    conv_bc,
    conv_bc_bias,
    dt_bias,
    a_log,
    d_skip,
    gate_norm,
    w_out,
):
    batch_count, tokens_here, width = hidden.shape
    row_total = batch_count * tokens_here
    head_group = lax.axis_size("head")
    share_rows = row_total // head_group
    first_share = lax.axis_index("head") * share_rows
    layer_total = w_out.shape[0]
    inner_here = w_out.shape[1]
    heads_here = dt_bias.shape[1]
    head_size = inner_here // heads_here
    state_size = w_in_bc.shape[2] // 2
    inner_total = inner_here * head_group
    rim_rows = conv_x.shape[1] - 1
    stream_full = hidden.astype(jnp.float32).reshape(row_total, width)
    stream_share = lax.dynamic_slice_in_dim(stream_full, first_share, share_rows, 0)
    normed_in = (
        rms_scale(stream_full, norm_gain[0])
        .astype(jnp.bfloat16)
        .reshape(batch_count, tokens_here, width)
    )
    stored = []
    for layer_index in range(layer_total):
        projected = jnp.einsum(
            "btd,dki->btki", normed_in, w_in_zx[layer_index], preferred_element_type=jnp.float32
        )
        gate_in = projected[:, :, 0]
        values_raw = projected[:, :, 1].astype(jnp.bfloat16)
        states_raw = jnp.einsum(
            "btd,dn->btn", normed_in, w_in_bc[layer_index], preferred_element_type=jnp.float32
        ).astype(jnp.bfloat16)
        steps_raw = jnp.einsum(
            "btd,dh->bth", normed_in, w_in_dt[layer_index], preferred_element_type=jnp.float32
        )
        joined = jnp.concatenate([values_raw, states_raw], -1)
        rim_part = shifted(joined[:, tokens_here - rim_rows :], "seq", 1)
        padded = jnp.concatenate([rim_part, joined], 1)
        kernel = jnp.concatenate([conv_x[layer_index], conv_bc[layer_index]], -1)
        offset = jnp.concatenate([conv_x_bias[layer_index], conv_bc_bias[layer_index]], -1)
        before_act = causal_apply(padded, kernel, offset, tokens_here)
        activated = jax.nn.silu(before_act).astype(jnp.bfloat16)
        inputs = (
            activated[..., :inner_here]
            .astype(jnp.float32)
            .reshape(batch_count, tokens_here, heads_here, head_size)
        )
        b_rows = activated[..., inner_here : inner_here + state_size].astype(jnp.float32)
        c_rows = activated[..., inner_here + state_size :].astype(jnp.float32)
        step_size = jax.nn.softplus(steps_raw + dt_bias[layer_index])
        log_decay = -jnp.exp(a_log[layer_index]) * step_size
        local_out, state_local = ssd_parts(inputs, step_size, log_decay, b_rows, c_rows, True)
        cumulative = jnp.cumsum(log_decay, axis=1)
        decay_total = jnp.exp(cumulative[:, -1])
        chained = entering(
            (decay_total, state_local),
            "seq",
            chain_combine,
            (jnp.ones_like(decay_total), jnp.zeros_like(state_local)),
            False,
        )
        state_in = chained[1]
        mixed = (
            local_out
            + jnp.exp(cumulative)[..., None]
            * jnp.einsum("btn,bhpn->bthp", c_rows, state_in, precision=PRECISE)
            + d_skip[layer_index][:, None] * inputs
        )
        mixed_flat = mixed.reshape(batch_count, tokens_here, inner_here)
        gated = mixed_flat * jax.nn.silu(gate_in)
        square_sum = lax.psum(jnp.sum(gated * gated, -1), "head")
        gate_rstd = lax.rsqrt(square_sum / inner_total + EPSILON)
        normed_rows = (
            (gated * gate_rstd[..., None] * gate_norm[layer_index])
            .astype(jnp.bfloat16)
            .reshape(row_total, inner_here)
        )
        out_weight = w_out[layer_index]
        branch_share = lax.psum_scatter(
            jnp.dot(normed_rows, out_weight, preferred_element_type=jnp.float32),
            "head",
            scatter_dimension=0,
            tiled=True,
        )
        stored.append(
            {
                "normed_in": normed_in,
                "stream_share": stream_share,
                "gate_in": gate_in,
                "padded": padded,
                "kernel": kernel,
                "before_act": before_act,
                "inputs": inputs,
                "steps_raw": steps_raw,
                "b_rows": b_rows,
                "c_rows": c_rows,
                "cumulative": cumulative,
                "decay_total": decay_total,
                "state_in": state_in,
                "mixed_flat": mixed_flat,
                "gated": gated,
                "gate_rstd": gate_rstd,
                "normed_rows": normed_rows,
            }
        )
        stream_share = stream_share + branch_share
        if layer_index + 1 < layer_total:
            stream_full = gather_stream(stream_share)
            normed_in = (
                rms_scale(stream_full, norm_gain[layer_index + 1])
                .astype(jnp.bfloat16)
                .reshape(batch_count, tokens_here, width)
            )
    final_out = gather_stream(stream_share).reshape(batch_count, tokens_here, width)
    grad_full = cotangent.astype(jnp.float32).reshape(row_total, width)
    layer_grads = [None] * layer_total
    for layer_index in range(layer_total - 1, -1, -1):
        saved_layer = stored[layer_index]
        gated = saved_layer["gated"]
        gate_rstd = saved_layer["gate_rstd"]
        gate_in = saved_layer["gate_in"]
        before_act = saved_layer["before_act"]
        kernel = saved_layer["kernel"]
        padded = saved_layer["padded"]
        normed_in = saved_layer["normed_in"]
        grad_out = grad_full.astype(jnp.bfloat16)
        grad_wout = jnp.einsum(
            "ri,rd->id", saved_layer["normed_rows"], grad_out, preferred_element_type=jnp.float32
        )
        grad_normed = jnp.einsum(
            "rd,id->ri", grad_out, w_out[layer_index], preferred_element_type=jnp.float32
        ).reshape(batch_count, tokens_here, inner_here)
        grad_gate_norm = jnp.sum(grad_normed * gated * gate_rstd[..., None], (0, 1))
        weighted = grad_normed * gate_norm[layer_index]
        cross_sum = lax.psum(jnp.sum(weighted * gated, -1), "head")
        grad_gated = (
            gate_rstd[..., None] * weighted
            - gated * (gate_rstd**3 * cross_sum / inner_total)[..., None]
        )
        sigmoid_gate = jax.nn.sigmoid(gate_in)
        grad_mixed = (grad_gated * gate_in * sigmoid_gate).reshape(
            batch_count, tokens_here, heads_here, head_size
        )
        grad_gate = (
            grad_gated
            * saved_layer["mixed_flat"]
            * sigmoid_gate
            * (1.0 + gate_in * (1.0 - sigmoid_gate))
        )
        decay_total = saved_layer["decay_total"]
        c_rows = saved_layer["c_rows"]
        grad_local = jnp.einsum(
            "bthp,btn->bhpn",
            jnp.exp(saved_layer["cumulative"])[..., None] * grad_mixed,
            c_rows,
            precision=PRECISE,
        )
        returned = entering(
            (decay_total, grad_local),
            "seq",
            back_combine,
            (jnp.ones_like(decay_total), jnp.zeros_like(grad_local)),
            True,
        )
        unused_out, pullback = jax.vjp(
            ssd_device,
            saved_layer["inputs"],
            saved_layer["steps_raw"],
            dt_bias[layer_index],
            a_log[layer_index],
            d_skip[layer_index],
            saved_layer["b_rows"],
            c_rows,
            saved_layer["state_in"],
        )
        (
            grad_inputs,
            grad_steps,
            grad_dt_bias,
            grad_a_log,
            grad_d_skip,
            grad_b_rows,
            grad_c_rows,
            unused_state,
        ) = pullback((grad_mixed, returned[1]))
        grad_states = lax.psum(jnp.concatenate([grad_b_rows, grad_c_rows], -1), "head")
        grad_act = jnp.concatenate(
            [grad_inputs.reshape(batch_count, tokens_here, inner_here), grad_states], -1
        )
        sigmoid_pre = jax.nn.sigmoid(before_act)
        grad_pre = grad_act * sigmoid_pre * (1.0 + before_act * (1.0 - sigmoid_pre))
        ahead = shifted(grad_pre[:, :rim_rows], "seq", -1)
        extended = jnp.concatenate([grad_pre, ahead], 1)
        grad_joined = kernel[0] * extended[:, rim_rows : rim_rows + tokens_here]
        for tap_index in range(1, rim_rows + 1):
            grad_joined = (
                grad_joined
                + kernel[tap_index]
                * extended[:, rim_rows - tap_index : rim_rows - tap_index + tokens_here]
            )
        grad_kernel = jnp.stack(
            [
                jnp.sum(
                    grad_pre * padded[:, tap_index : tap_index + tokens_here].astype(jnp.float32),
                    (0, 1),
                )
                for tap_index in range(rim_rows + 1)
            ]
        )
        grad_offset = jnp.sum(grad_pre, (0, 1))
        grad_proj = jnp.stack([grad_gate, grad_joined[..., :inner_here]], 2).astype(jnp.bfloat16)
        grad_state_raw = grad_joined[..., inner_here:].astype(jnp.bfloat16)
        grad_steps_low = grad_steps.astype(jnp.bfloat16)
        grad_wzx = jnp.einsum(
            "btd,btki->dki", normed_in, grad_proj, preferred_element_type=jnp.float32
        )
        grad_wdt = jnp.einsum(
            "btd,bth->dh", normed_in, grad_steps_low, preferred_element_type=jnp.float32
        )
        grad_wbc = jnp.einsum(
            "btd,btn->dn", normed_in, grad_state_raw, preferred_element_type=jnp.float32
        )
        proj_rows = grad_proj.reshape(row_total, 2, inner_here)
        step_rows = grad_steps_low.reshape(row_total, heads_here)
        zx_weight = w_in_zx[layer_index]
        step_weight = w_in_dt[layer_index]
        grad_normed_in = lax.psum_scatter(
            jnp.einsum("rki,dki->rd", proj_rows, zx_weight, preferred_element_type=jnp.float32)
            + jnp.einsum("rh,dh->rd", step_rows, step_weight, preferred_element_type=jnp.float32),
            "head",
            scatter_dimension=0,
            tiled=True,
        )
        state_share = lax.dynamic_slice_in_dim(
            grad_state_raw.reshape(row_total, 2 * state_size), first_share, share_rows, 0
        )
        grad_normed_in = grad_normed_in + jnp.einsum(
            "rn,dn->rd", state_share, w_in_bc[layer_index], preferred_element_type=jnp.float32
        )
        stream_in = saved_layer["stream_share"]
        input_rstd = lax.rsqrt(jnp.mean(stream_in * stream_in, -1, keepdims=True) + EPSILON)
        gain_part = jnp.sum(grad_normed_in * stream_in * input_rstd, 0)
        weighted_in = grad_normed_in * norm_gain[layer_index]
        residual_share = lax.dynamic_slice_in_dim(grad_full, first_share, share_rows, 0)
        grad_share = (
            input_rstd * weighted_in
            - stream_in
            * input_rstd**3
            * jnp.sum(weighted_in * stream_in, -1, keepdims=True)
            / width
            + residual_share
        )
        gathered = (
            lax.all_gather(for_sending(grad_share), "head", axis=0, tiled=True).astype(
                grad_share.dtype
            ),
            lax.all_gather(gain_part[None].astype(jnp.bfloat16), "head", axis=0, tiled=True).astype(
                jnp.float32
            ),
        )
        grad_full = gathered[0]
        grad_norm_gain = jnp.sum(gathered[1], 0)
        local_grads = (
            grad_norm_gain,
            grad_wzx,
            grad_wdt,
            grad_wbc,
            grad_kernel[:, :inner_here],
            grad_offset[:inner_here],
            grad_kernel[:, inner_here:],
            grad_offset[inner_here:],
            grad_dt_bias,
            grad_a_log,
            grad_d_skip,
            grad_gate_norm,
            grad_wout,
        )
        local_grads = (
            lax.psum(local_grads[0].astype(jnp.bfloat16), "seq").astype(jnp.float32),
            lax.psum(local_grads[1].astype(jnp.bfloat16), "seq").astype(jnp.float32),
            lax.psum(local_grads[2].astype(jnp.bfloat16), "seq").astype(jnp.float32),
            lax.psum(local_grads[3].astype(jnp.bfloat16), "seq").astype(jnp.float32),
            lax.psum(local_grads[4].astype(jnp.bfloat16), "seq").astype(jnp.float32),
            lax.psum(local_grads[5].astype(jnp.bfloat16), "seq").astype(jnp.float32),
            lax.psum(local_grads[6].astype(jnp.bfloat16), "seq").astype(jnp.float32),
            lax.psum(local_grads[7].astype(jnp.bfloat16), "seq").astype(jnp.float32),
            lax.psum(local_grads[8].astype(jnp.bfloat16), "seq").astype(jnp.float32),
            lax.psum(local_grads[9].astype(jnp.bfloat16), "seq").astype(jnp.float32),
            lax.psum(local_grads[10].astype(jnp.bfloat16), "seq").astype(jnp.float32),
            lax.psum(local_grads[11].astype(jnp.bfloat16), "seq").astype(jnp.float32),
            lax.psum(local_grads[12].astype(jnp.bfloat16), "seq").astype(jnp.float32),
        )
        layer_grads[layer_index] = local_grads
    stacked = [
        jnp.stack([layer_grads[depth_index][slot_index] for depth_index in range(layer_total)])
        for slot_index in range(13)
    ]
    hidden_grad = grad_full.reshape(batch_count, tokens_here, width)
    return (
        final_out,
        hidden_grad,
        stacked[0],
        stacked[1],
        stacked[2],
        stacked[3],
        stacked[4],
        stacked[5],
        stacked[6],
        stacked[7],
        stacked[8],
        stacked[9],
        stacked[10],
        stacked[11],
        stacked[12],
    )


def solution(mesh):
    placed = (
        P(None, "seq", None),
        P(None, "seq", None),
        P(),
        P(None, None, None, "head"),
        P(None, None, "head"),
        P(),
        P(None, None, "head"),
        P(None, "head"),
        P(),
        P(),
        P(None, "head"),
        P(None, "head"),
        P(None, "head"),
        P(None, "head"),
        P(None, "head", None),
    )
    return jax.shard_map(
        shards,
        mesh=mesh,
        in_specs=placed,
        out_specs=(
            P(None, "seq", None),
            P(None, "seq", None),
            P(),
            P(None, None, None, "head"),
            P(None, None, "head"),
            P(),
            P(None, None, "head"),
            P(None, "head"),
            P(),
            P(),
            P(None, "head"),
            P(None, "head"),
            P(None, "head"),
            P(None, "head"),
            P(None, "head", None),
        ),
        check_vma=False,
    )
```

profile of v0, /device:TPU:0, one launch (start us, length us, event | category | flops | bytes accessed | tf_op | source)
XLA Modules:
  0.0 875.9 jit_solution(9967429833535025608)
XLA Ops:
  51.9 16.2 %all-gather.21.cloned.1.call-done = f32[16,6,64,128]{3,2,1,0:T(8,128)} async-done(((f32[2,6,64,128]{3,2,1,0:T(8,128)}), f32[16,6,64,128]{3,2,1,0:T(8,128)}) %all-gather.21.cloned.1.call-update) | async-done | bytes 3145744 | tf_op jit(solution)/shard_map/all_gather | solution.py:20
  74.3 12.0 %psum.224 = f32[2,256]{1,0:T(2,128)S(1)} all-reduce(f32[2,256]{1,0:T(2,128)S(1)} %get-tuple-element.515), channel_id=1, replica_groups=mesh['seq'=8,'head'=4] {'head'}, use_global_device_ids=true, to_apply=%region_6.7 | all-reduce | flops 512 | bytes 4096 | tf_op jit(solution)/shard_map/psum | solution.py:197
  91.8 38.6 %reduce-scatter.5.cloned.1.call-done = f32[128,768]{1,0:T(8,128)} async-done(((f32[512,768]{1,0:T(8,128)}), f32[128,768]{1,0:T(8,128)}) %reduce-scatter.5.cloned.1.call-update) | async-done | bytes 393232 | tf_op jit(solution)/shard_map/reduce_scatter | solution.py:205
  134.1 34.7 %all-gather.17.cloned.1.call-done = f32[512,768]{1,0:T(8,128)} async-done(((f32[128,768]{1,0:T(8,128)}), f32[512,768]{1,0:T(8,128)}) %all-gather.17.cloned.1.call-update) | async-done | bytes 1572880 | tf_op jit(solution)/shard_map/all_gather | solution.py:110
  197.3 12.5 %all-gather.2 = f32[16,1,6]{2,1,0:T(1,128)S(1)} all-gather(f32[2,1,6]{2,1,0:T(1,128)S(1)} %bitcast.750), channel_id=4, replica_groups=mesh['seq'=8,'head'=4] {'seq'}, dimensions={0}, use_global_device_ids=true | all-gather | bytes 432 | tf_op jit(solution)/shard_map/all_gather | solution.py:20
  248.6 18.8 %psum.226 = f32[2,256]{1,0:T(2,128)S(1)} all-reduce(f32[2,256]{1,0:T(2,128)S(1)} %get-tuple-element.384), channel_id=1, replica_groups=mesh['seq'=8,'head'=4] {'head'}, use_global_device_ids=true, to_apply=%region_19.20 | all-reduce | flops 512 | bytes 4096 | tf_op jit(solution)/shard_map/psum | solution.py:261
  293.6 19.4 %all-gather.25.cloned.1.call-done = f32[16,6,64,128]{3,2,1,0:T(8,128)} async-done(((f32[2,6,64,128]{3,2,1,0:T(8,128)}), f32[16,6,64,128]{3,2,1,0:T(8,128)}) %all-gather.25.cloned.1.call-update) | async-done | bytes 3145744 | tf_op jit(solution)/shard_map/all_gather | solution.py:20
  330.5 15.1 %reduce-window.66 = f32[2,6,2,128]{3,2,1,0:T(2,128)S(1)} reduce-window(f32[2,6,2,128]{3,2,1,0:T(2,128)S(1)} %copy.615, f32[]{:T(128)} %constant.159.clone.1), window={size=1x1x1x128 pad=0_0x0_0x0_0x0_127}, to_apply=%region_36.38 | reduce-window | flops 390144 | bytes 24580 | tf_op jit(solution)/shard_map/reduce-window.8
  346.9 15.1 %reduce-window.64 = f32[2,6,2,128]{3,2,1,0:T(2,128)S(1)} reduce-window(f32[2,6,2,128]{3,2,1,0:T(2,128)S(1)} %copy.607, f32[]{:T(128)} %constant.159.clone.1), window={size=1x1x1x128 pad=0_0x0_0x0_0x0_127}, to_apply=%region_29.31 | reduce-window | flops 390144 | bytes 24580 | tf_op jit(solution)/shard_map/reduce-window.6
  387.8 29.8 %all-reduce.10.cloned.1.call-done = f32[2,256,256]{2,1,0:T(8,128)} async-done(((f32[2,256,256]{2,1,0:T(8,128)}), f32[2,256,256]{2,1,0:T(8,128)}) %all-reduce.10.cloned.1.call-update) | async-done | bytes 524304 | tf_op jit(solution)/shard_map/psum | solution.py:312
  436.9 29.5 %reduce-scatter.9.cloned.1.call-done = f32[128,768]{1,0:T(8,128)} async-done(((f32[512,768]{1,0:T(8,128)}), f32[128,768]{1,0:T(8,128)}) %reduce-scatter.9.cloned.1.call-update) | async-done | bytes 393232 | tf_op jit(solution)/shard_map/reduce_scatter | solution.py:353
  468.4 35.1 %reduce-scatter.7.cloned.1.call-done = f32[128,768]{1,0:T(8,128)} async-done(((f32[512,768]{1,0:T(8,128)}), f32[128,768]{1,0:T(8,128)}) %reduce-scatter.7.cloned.1.call-update) | async-done | bytes 393232 | tf_op jit(solution)/shard_map/reduce_scatter | solution.py:205
  505.6 17.9 %all_gather.64 = bf16[512,768]{1,0:T(8,128)(2,1)S(1)} all-gather(bf16[128,768]{1,0:T(8,128)(2,1)S(1)} %get-tuple-element.530), channel_id=1, replica_groups=mesh['seq'=8,'head'=4] {'head'}, dimensions={0}, use_global_device_ids=true | all-gather | bytes 983040 | tf_op jit(solution)/shard_map/all_gather | solution.py:380
  559.9 14.0 %all-gather.27.cloned.1.call-done = f32[16,6,64,128]{3,2,1,0:T(8,128)} async-done(((f32[2,6,64,128]{3,2,1,0:T(8,128)}), f32[16,6,64,128]{3,2,1,0:T(8,128)}) %all-gather.27.cloned.1.call-update) | async-done | bytes 3145744 | tf_op jit(solution)/shard_map/all_gather | solution.py:20
  574.0 12.9 %while.55 = (s32[]{:T(128)}, f32[2,6,64,128]{3,2,1,0:T(8,128)S(1)}, s32[]{:T(128)}, f32[8,2,6,64,128]{4,3,2,1,0:T(8,128)}, f32[8,2,6]{2,1,0:T(2,128)}, /*index=5*/s32[]{:T(128)}, s32[]{:T(128)}, s32[]{:T(128)}, s32[]{:T(128)}) while((s32[]{:T(128)}, f32[2,6,64,128]{3,2,1,0:T(8,128)S(1)}, s32[]{:T(128)}, f32[8,2,6,64,128]{4,3,2,1,0:T(8,128)}, ...), condition=%wide.region_43.45_spmd, body=%wide.region_42.44_spmd.sunk | while | flops 196614 | bytes 1179939 | solution.py:29
  619.5 23.5 %all-reduce.12.cloned.1.call-done = f32[2,256,256]{2,1,0:T(8,128)} async-done(((f32[2,256,256]{2,1,0:T(8,128)}), f32[2,256,256]{2,1,0:T(8,128)}) %all-reduce.12.cloned.1.call-update) | async-done | bytes 524304 | tf_op jit(solution)/shard_map/psum | solution.py:312
  658.7 15.1 %reduce-window.76 = f32[2,6,2,128]{3,2,1,0:T(2,128)S(1)} reduce-window(f32[2,6,2,128]{3,2,1,0:T(2,128)S(1)} %copy.656, f32[]{:T(128)} %constant.159.clone.1), window={size=1x1x1x128 pad=0_0x0_0x0_0x0_127}, to_apply=%region_58.60 | reduce-window | flops 390144 | bytes 24580 | tf_op jit(solution)/shard_map/reduce-window.14
  675.1 15.1 %reduce-window.74 = f32[2,6,2,128]{3,2,1,0:T(2,128)S(1)} reduce-window(f32[2,6,2,128]{3,2,1,0:T(2,128)S(1)} %copy.648, f32[]{:T(128)} %constant.159.clone.1), window={size=1x1x1x128 pad=0_0x0_0x0_0x0_127}, to_apply=%region_51.53 | reduce-window | flops 390144 | bytes 24580 | tf_op jit(solution)/shard_map/reduce-window.12
  700.6 13.1 %all-gather.9 = bf16[4,1,768]{2,1,0:T(2,128)(2,1)S(1)} all-gather(bf16[1,1,768]{2,1,0:T(2,128)(2,1)S(1)} %reshape.567), channel_id=9, replica_groups=mesh['seq'=8,'head'=4] {'head'}, dimensions={0}, use_global_device_ids=true | all-gather | bytes 7680 | tf_op jit(solution)/shard_map/all_gather | solution.py:383
  714.5 52.8 %all-reduce.14.cloned.1.call-done = (bf16[1,768,2,384]{3,1,2,0:T(8,128)(2,1)}, bf16[1,768,2,384]{3,1,2,0:T(8,128)(2,1)}, bf16[1,768,256]{2,1,0:T(8,128)(2,1)}, b...) async-done(((bf16[1,768,2,384]{3,1,2,0:T(8,128)(2,1)}, bf16[1,768,2,384]{3,1,2,0:T(8,128)(2,1)}, ...) | async-done | bytes 4325392 | tf_op jit(solution)/shard_map/psum | solution.py:406
  778.5 27.3 %reduce-scatter.11.cloned.1.call-done = f32[128,768]{1,0:T(8,128)} async-done(((f32[512,768]{1,0:T(8,128)}), f32[128,768]{1,0:T(8,128)}) %reduce-scatter.11.cloned.1.call-update) | async-done | bytes 393232 | tf_op jit(solution)/shard_map/reduce_scatter | solution.py:353
  807.2 13.1 %all-gather.8 = bf16[4,1,768]{2,1,0:T(2,128)(2,1)S(1)} all-gather(bf16[1,1,768]{2,1,0:T(2,128)(2,1)S(1)} %reshape.565), channel_id=8, replica_groups=mesh['seq'=8,'head'=4] {'head'}, dimensions={0}, use_global_device_ids=true | all-gather | bytes 7680 | tf_op jit(solution)/shard_map/all_gather | solution.py:383
  820.4 22.9 %all-reduce.4 = (bf16[1,768]{1,0:T(2,128)(2,1)S(1)}, bf16[1,768]{1,0:T(2,128)(2,1)S(1)}, bf16[1,768,6]{1,2,0:T(8,128)(2,1)S(1)}, bf16[1,768,6]{1,2,0:T(8,128)(2,...) all-reduce(bf16[1,768]{1,0:T(2,128)(2,1)S(1)} %stack.255, ...), channel_id=1, replica_groups=mesh['seq'=8,'head'=4] {'seq'}, use_global_device_ids=true, to_apply=%region_67.69 | all-reduce | flops 17956 | bytes 71824 | tf_op jit(solution)/shard_map/psum | solution.py:405
  845.1 17.4 %all_gather.67 = bf16[512,768]{1,0:T(8,128)(2,1)S(1)} all-gather(bf16[128,768]{1,0:T(8,128)(2,1)S(1)} %add_convert_fusion), channel_id=1, replica_groups=mesh['seq'=8,'head'=4] {'head'}, dimensions={0}, use_global_device_ids=true | all-gather | bytes 983040 | tf_op jit(solution)/shard_map/all_gather | solution.py:380
  (732 shorter events, 358.2 us)
Async XLA Ops:
  7.2 61.0 %all-gather.21.cloned.1.call-start = ((), (), s32[]{:S(2)}) async-start(), calls=%async_computation.12 | async-start | bytes 3538944 | tf_op jit(solution)/shard_map/all_gather | solution.py:20
  15.9 13.6 %collective-permute-start = (bf16[2,3,640]{2,1,0:T(4,128)(2,1)S(1)}, bf16[2,3,640]{2,1,0:T(4,128)(2,1)S(1)}, u32[]{:S(2)}, u32[]{:S(2)}) collective-permute-start(bf16[2,3,640]{2,1,0:T(4,128)(2,1)S(1)} %fusion.304), channel_id=1, source_target_pairs={{0,4},{4,8},{8,12},{12,16},{16,20},{20,24},{24,28},{1,5},{5,9},{9,... | collective-permute-start | bytes 23048 | tf_op jit(solution)/shard_map/ppermute | solution.py:13
  33.3 97.1 %reduce-scatter.5.cloned.1.call-start = ((), (), s32[]{:S(2)}) async-start(), calls=%async_computation.4 | async-start | bytes 1966080 | tf_op jit(solution)/shard_map/reduce_scatter | solution.py:205
  90.5 78.3 %all-gather.17.cloned.1.call-start = ((), (), s32[]{:S(2)}) async-start(), calls=%async_computation.5 | async-start | bytes 1966080 | tf_op jit(solution)/shard_map/all_gather | solution.py:110
  91.7 78.8 %copy-start.20 = (f32[512,768]{1,0:T(8,128)}, f32[512,768]{1,0:T(8,128)S(1)}, u32[]{:S(2)}) copy-start(f32[512,768]{1,0:T(8,128)S(1)} %convert.136) | copy-start | bytes 4718596
  91.8 41.7 %copy-start.137 = (f32[384]{0:T(512)S(1)}, f32[384]{0:T(512)}, u32[]{:S(2)}) copy-start(f32[384]{0:T(512)} %get-tuple-element.425) | copy-start | bytes 4612
  91.8 41.7 %copy-start.154 = (f32[1,256]{1,0:T(1,128)S(1)}, f32[1,256]{1,0:T(1,128)}, u32[]{:S(2)}) copy-start(f32[1,256]{1,0:T(1,128)} %get-tuple-element.560) | copy-start | bytes 3076
  132.8 91.4 %all-gather.23.cloned.1.call-start = ((), (), s32[]{:S(2)}) async-start(), calls=%async_computation.13 | async-start | bytes 3538944 | tf_op jit(solution)/shard_map/all_gather | solution.py:20
  183.1 2.5 collective-permute-start.1
  186.7 80.6 %copy-start.2 = (bf16[2,256,640]{2,1,0:T(8,128)(2,1)}, bf16[2,256,640]{2,1,0:T(8,128)(2,1)S(1)}, u32[]{:S(2)}) copy-start(bf16[2,256,640]{2,1,0:T(8,128)(2,1)S(1)} %multiply_convert_fusion.2) | copy-start | bytes 1966084
  189.1 97.2 %copy-start.17 = (bf16[2,256,384]{1,2,0:T(8,128)(2,1)}, bf16[2,256,384]{1,2,0:T(8,128)(2,1)S(1)}, u32[]{:S(2)}) copy-start(bf16[2,256,384]{1,2,0:T(8,128)(2,1)S(1)} %copy.563) | copy-start | bytes 1179652
  190.4 122.5 %all-gather.25.cloned.1.call-start = ((), (), s32[]{:S(2)}) async-start(), calls=%async_computation.14 | async-start | bytes 3538944 | tf_op jit(solution)/shard_map/all_gather | solution.py:20
  274.9 142.7 %all-reduce.10.cloned.1.call-start = ((), (), s32[]{:S(2)}) async-start(), calls=%async_computation.8 | async-start | bytes 1048576 | tf_op jit(solution)/shard_map/psum | solution.py:312
  379.8 86.5 %reduce-scatter.9.cloned.1.call-start = ((), (), s32[]{:S(2)}) async-start(), calls=%async_computation.9 | async-start | bytes 1966080 | tf_op jit(solution)/shard_map/reduce_scatter | solution.py:353
  421.0 3.1 collective-permute-start.2
  430.3 73.2 %reduce-scatter.7.cloned.1.call-start = ((), (), s32[]{:S(2)}) async-start(), calls=%async_computation.6 | async-start | bytes 1966080 | tf_op jit(solution)/shard_map/reduce_scatter | solution.py:205
  434.6 139.4 %all-gather.27.cloned.1.call-start = ((), (), s32[]{:S(2)}) async-start(), calls=%async_computation.15 | async-start | bytes 3538944 | tf_op jit(solution)/shard_map/all_gather | solution.py:20
  543.5 99.4 %all-reduce.12.cloned.1.call-start = ((), (), s32[]{:S(2)}) async-start(), calls=%async_computation.10 | async-start | bytes 1048576 | tf_op jit(solution)/shard_map/psum | solution.py:312
  605.1 108.8 %all-gather.19.cloned.1.call-start = ((), (), s32[]{:S(2)}) async-start(), calls=%async_computation.7 | async-start | bytes 1966080 | tf_op jit(solution)/shard_map/all_gather | solution.py:110
  610.6 156.7 %all-reduce.14.cloned.1.call-start = ((), (), s32[]{:S(2)}) async-start(), calls=%async_computation.16 | async-start | bytes 8650752 | tf_op jit(solution)/shard_map/psum | solution.py:406
  645.7 3.1 collective-permute-start.3
  649.7 64.8 %copy-start.23 = (bf16[2,256,640]{2,1,0:T(8,128)(2,1)}, bf16[2,256,640]{2,1,0:T(8,128)(2,1)S(1)}, u32[]{:S(2)}) copy-start(bf16[2,256,640]{2,1,0:T(8,128)(2,1)S(1)} %fusion.76) | copy-start | bytes 1966084
  653.1 152.7 %reduce-scatter.11.cloned.1.call-start = ((), (), s32[]{:S(2)}) async-start(), calls=%async_computation.11 | async-start | bytes 1966080 | tf_op jit(solution)/shard_map/reduce_scatter | solution.py:353
  778.4 41.9 %copy-start.157 = (bf16[6]{0:T(256)(128)(2,1)S(1)}, bf16[6]{0:T(256)(128)(2,1)}, u32[]{:S(2)}) copy-start(bf16[6]{0:T(256)(128)(2,1)} %get-tuple-element.499) | copy-start | bytes 40
  (165 other events, 1631.1 us)
Sparse Core Ops, SparseCore 0:
  33.4 34.7 all-gather.20
  90.6 39.6 reduce-scatter.4
  132.9 35.8 all-gather.16
  190.6 33.5 all-gather.22
  275.0 37.8 all-gather.24
  379.9 37.6 all-reduce.9
  430.4 35.8 reduce-scatter.8
  469.2 34.2 reduce-scatter.6
  543.6 30.2 all-gather.26
  605.2 37.6 all-reduce.11
  644.5 36.8 all-gather.18
  685.8 81.4 all-reduce.13
  770.1 35.6 reduce-scatter.10
where the time goes:
time: 888 us; the launch traced here: 876 us
  waiting for transfers between devices  332 us (37%)
  other arithmetic  162 us (18%)
  blocking collectives  159 us (18%)
  matrix products  103 us (12%)
  local copies, waits for them, and re-layouts  94.5 us (11%)
  between operations  16.6 us (2%)
    another operation x22, other arithmetic  75.6 us
    reduce_scatter x2, waiting for transfers between devices, shards(): lax.psum_scatter(jnp.dot(normed_rows, out_weight, preferred_element_type=...  73.7 us
    all_gather x4, waiting for transfers between devices, entering(): gathered = jax.tree.map(lambda a: lax.all_gather(a, axis), part)  59.3 us
    reduce_scatter x2, waiting for transfers between devices, shards(): lax.psum_scatter(jnp.einsum('rki,dki->rd', proj_rows, zx_weight, preferre...  56.8 us
    psum x2, waiting for transfers between devices, shards(): lax.psum(jnp.concatenate([grad_b_rows, grad_c_rows], -1), 'head')  53.2 us
    psum x1, waiting for transfers between devices, shards(): lax.psum(local_grads[1].astype(jnp.bfloat16), 'seq').astype(jnp.float32)  52.8 us
    all_gather x2, blocking collectives, shards(): lax.all_gather(for_sending(grad_share), 'head', axis=0, tiled=True)  35.3 us
    all_gather x2, waiting for transfers between devices, gather_stream(): return lax.all_gather(stream_part, 'head', axis=0, tiled=True)  34.7 us
  transfers between devices with their start and end apart: 17, of which 14 were waited for; matrix products, arithmetic and copies ran while one was open for 18% of the time, Pallas kernels for 0%

commit v1 on v0

v1 whole, which is shorter than its diff:
```python
import jax
import jax.numpy as jnp
from jax import lax
from jax.experimental import pallas as pl
from jax.experimental.pallas import tpu as pltpu
from jax.sharding import PartitionSpec as P

EPSILON = 1e-05
PRECISE = lax.Precision.HIGHEST
LANES = 128
HALO = 16
F32 = jnp.float32
BF16 = jnp.bfloat16


def nn(a, b, precision=None):
    return lax.dot_general(
        a, b, (((1,), (0,)), ((), ())), precision=precision, preferred_element_type=F32
    )


def nt(a, b, precision=None):
    return lax.dot_general(
        a, b, (((1,), (1,)), ((), ())), precision=precision, preferred_element_type=F32
    )


def tn(a, b, precision=None):
    return lax.dot_general(
        a, b, (((0,), (0,)), ((), ())), precision=precision, preferred_element_type=F32
    )


def iota(shape, axis):
    return lax.broadcasted_iota(jnp.int32, shape, axis)


def sigmoid(v):
    return 1.0 / (1.0 + jnp.exp(-v))


def softplus(v):
    small = jnp.exp(-jnp.abs(v))
    grown = 1.0 + small
    gap = grown - 1.0
    log1p = jnp.where(gap == 0.0, small, jnp.log(grown) * small / jnp.where(gap == 0.0, 1.0, gap))
    return jnp.maximum(v, 0.0) + log1p


def spread_heads(inner, head_size):
    return (iota((LANES, inner), 1) // head_size == iota((LANES, inner), 0)).astype(F32)


def lower_tri(length):
    return (iota((length, length), 0) >= iota((length, length), 1)).astype(F32)


def call(kernel, outs, args, specs=None, scratch=(), prefetch=None):
    whole = lambda a: pl.BlockSpec(a.shape, lambda *_, n=a.ndim: (0,) * n)
    in_specs = [whole(a) if s is None else s for a, s in zip(args, specs or [None] * len(args))]
    out_shape = [jax.ShapeDtypeStruct(s, d) for s, d in outs]
    return pl.pallas_call(
        kernel,
        grid_spec=pltpu.PrefetchScalarGridSpec(
            num_scalar_prefetch=0 if prefetch is None else 1,
            grid=(1,),
            in_specs=in_specs,
            out_specs=[whole(o) for o in out_shape],
            scratch_shapes=list(scratch),
        ),
        out_shape=out_shape,
    )(*(() if prefetch is None else (prefetch,)), *args)


def layer_spec(array, layer, extra=None):
    shape = (None,) + array.shape[1:]
    index = (layer,) + (0,) * (array.ndim - 1)
    if extra is not None:
        shape = (None, None) + array.shape[2:]
        index = (layer, extra) + (0,) * (array.ndim - 2)
    return pl.BlockSpec(shape, lambda *_: index)


def forward_kernel(dims):
    batch, length, inner, heads, head_size, state = dims

    def kernel(
        normed, halo, w_gate, w_val, w_bc, w_dt, taps_x, taps_bc, head_par,
        gate_out, padx_out, padbc_out, prex_out, prebc_out, local_out, step_out, cum_out, pay_out,
        y_buf,
    ):
        spread = spread_heads(inner, head_size)
        tri = lower_tri(length)
        causal = iota((length, length), 0) >= iota((length, length), 1)
        rates = -jnp.exp(head_par[1:2])
        skip = nn(head_par[...], spread, PRECISE)[2:3]
        extra = jnp.zeros((1, LANES), F32)
        for b in range(batch):
            rows = slice(b * length, (b + 1) * length)
            x_in = normed[rows]
            x_halo = halo[b * HALO : (b + 1) * HALO]
            gate_out[rows] = nn(x_in, w_gate[...])
            acts = []
            for weight, taps, pad_out, pre_out in (
                (w_val, taps_x, padx_out, prex_out),
                (w_bc, taps_bc, padbc_out, prebc_out),
            ):
                base = b * (length + 8)
                pad_out[base : base + 8] = nn(x_halo, weight[...])[HALO - 8 :].astype(BF16).astype(F32)
                pad_out[base + 8 : base + 8 + length] = nn(x_in, weight[...]).astype(BF16).astype(F32)
                pre = taps[4:5] + taps[0:1] * pad_out[base + 5 : base + 5 + length]
                for k in range(1, 4):
                    pre = pre + taps[k : k + 1] * pad_out[base + 5 + k : base + 5 + k + length]
                pre_out[rows] = pre
                acts.append((pre * sigmoid(pre)).astype(BF16))
            x_act, bc = acts
            b_rows, c_rows = bc[:, :state], bc[:, state:]
            step_raw = nn(x_in, w_dt[...]) + head_par[0:1]
            step = softplus(step_raw)
            cum = nn(tri, rates * step, PRECISE)
            step_out[rows] = step_raw
            cum_out[rows] = cum
            total = cum[length - 1 : length]
            x32 = x_act.astype(F32)
            step_x = nn(step, spread, PRECISE) * x32
            tail = nn(jnp.exp(total - cum), spread, PRECISE)
            pay_out[:, b * inner : (b + 1) * inner] = tn(b_rows, (tail * step_x).astype(BF16)).astype(BF16)
            place = (iota((LANES, LANES), 1) == iota((LANES, LANES), 0) + b * heads) & (
                iota((LANES, LANES), 0) < heads
            )
            extra = extra + nn(jnp.exp(jnp.broadcast_to(total, (8, LANES))), place.astype(F32), PRECISE)[0:1]
            step_xb = step_x.astype(BF16)
            scores = nt(c_rows, b_rows)
            cum_t = cum.T
            for h in range(heads):
                decay = jnp.exp(jnp.where(causal, cum[:, h : h + 1] - cum_t[h : h + 1, :], -1e30))
                y_buf[:, h * head_size : (h + 1) * head_size] = nn(
                    (scores * decay).astype(BF16), step_xb[:, h * head_size : (h + 1) * head_size]
                )
            local_out[rows] = y_buf[...] + skip * x32
        high = extra.astype(BF16).astype(F32)
        low = pltpu.roll(jnp.broadcast_to(extra - high, (8, LANES)), LANES // 2, 1)[0:1]
        lane = iota((1, LANES), 1)
        both = jnp.where(lane < LANES // 2, high, low)
        pay_out[:, batch * inner :] = jnp.broadcast_to(both, (state, LANES)).astype(BF16)

    return kernel


def decay_rows(extra, width, head_size):
    pick = (iota((LANES, width), 0) % (LANES // 2) == iota((LANES, width), 1) // head_size).astype(BF16)
    return nn(extra, pick)


def scan_kernel(head_size, reverse):
    def kernel(part, decays, entering):
        peers, rows, width = entering.shape
        state = jnp.zeros((rows, width), F32)
        order = range(peers - 1, -1, -1) if reverse else range(peers)
        for peer in order:
            entering[peer] = state.astype(BF16)
            decay = decay_rows(decays[peer][:, decays.shape[2] - LANES :], width, head_size)
            state = decay * state + part[peer][:, :width].astype(F32)

    return kernel


def mix_kernel(dims, final):
    batch, length, inner, heads, head_size, state = dims

    def kernel(local, gate, prebc, cum, entered, gate_norm, *rest):
        if final:
            cot, w_out, mixed_out, q_out, sums_out = rest
        else:
            mixed_out, q_out = rest
        spread = spread_heads(inner, head_size)
        ones = jnp.ones((8, inner), F32)
        sums = jnp.zeros((8, length), F32)
        for b in range(batch):
            rows = slice(b * length, (b + 1) * length)
            pre = prebc[rows, state:]
            c_rows = (pre * sigmoid(pre)).astype(BF16)
            carried = nn(c_rows, entered[:, b * inner : (b + 1) * inner])
            mixed = local[rows] + nn(jnp.exp(cum[rows]), spread, PRECISE) * carried
            mixed_out[rows] = mixed
            g = gate[rows]
            gated = mixed * g * sigmoid(g)
            weighted = gated * gate_norm[...]
            q_out[rows] = weighted.astype(BF16)
            if final:
                grad = nt(cot[rows], w_out[...])
                row = iota((8, length), 0)
                sums = jnp.where(row == 2 * b, nt(ones, gated * gated, PRECISE), sums)
                sums = jnp.where(row == 2 * b + 1, nt(ones, grad * weighted, PRECISE), sums)
        if final:
            sums_out[...] = sums

    return kernel


def out_kernel(dims, peers, inner_total, last):
    batch, length, inner, heads, head_size, state = dims

    def kernel(stream, gain, *rest):
        q, w, gn = rest[:peers], rest[peers : 2 * peers], rest[2 * peers : 3 * peers]
        outs = rest[3 * peers :]
        for b in range(batch):
            rows = slice(b * length, (b + 1) * length)
            total = jnp.zeros((length, 1), F32)
            u = None
            for p in range(peers):
                part = q[p][rows]
                gated = part.astype(F32) / gn[p][...]
                total = total + jnp.sum(gated * gated, 1, keepdims=True)
                term = nn(part, w[p][...])
                u = term if u is None else u + term
            rstd = lax.rsqrt(total / inner_total + EPSILON)
            after = stream[rows].astype(F32) + rstd * u
            outs[0][rows] = after
            if not last:
                scale = lax.rsqrt(jnp.mean(after * after, 1, keepdims=True) + EPSILON)
                outs[1][rows] = (after * scale * gain[...]).astype(BF16)
                outs[2][rows] = u
                outs[3][rows] = jnp.broadcast_to(rstd, (length, LANES))

    return kernel


def gate_back_kernel(dims, inner_total, last, peers):
    batch, length, inner, heads, head_size, state = dims

    def kernel(grad_out, w_out, mixed, gate, prebc, cum, gate_norm, *rest):
        sources, (dmix_out, dgate_out, normed_out, pay_out, gn_out) = rest[:-5], rest[-5:]
        spread = spread_heads(inner, head_size)
        gn_grad = jnp.zeros((1, inner), F32)
        if last:
            sums = sources[0][...]
            for s in sources[1:]:
                sums = sums + s[...]
            eye = (iota((length, length), 0) == iota((length, length), 1)).astype(F32)
            columns = nt(eye, sums, PRECISE)
        for b in range(batch):
            rows = slice(b * length, (b + 1) * length)
            go = grad_out[rows]
            if last:
                rstd = lax.rsqrt(columns[:, 2 * b : 2 * b + 1] / inner_total + EPSILON)
                cross = columns[:, 2 * b + 1 : 2 * b + 2]
            else:
                u, rstd_in = sources
                rstd = rstd_in[rows, 0:1]
                cross = jnp.sum(go.astype(F32) * u[rows], 1, keepdims=True)
            grad = nt(go, w_out[...])
            g = gate[rows]
            sig = sigmoid(g)
            silu = g * sig
            mix = mixed[rows]
            gated = mix * silu
            gn = gate_norm[...]
            normed_out[rows] = (gated * rstd * gn).astype(BF16)
            gn_grad = gn_grad + jnp.sum(grad * gated * rstd, 0, keepdims=True)
            dgated = rstd * gn * grad - gated * (rstd * rstd * rstd * cross / inner_total)
            dmix = dgated * silu
            dmix_out[rows] = dmix
            dgate_out[rows] = (dgated * mix * sig * (1.0 + g * (1.0 - sig))).astype(BF16)
            pre = prebc[rows, state:]
            c_rows = (pre * sigmoid(pre)).astype(BF16)
            grown = nn(jnp.exp(cum[rows]), spread, PRECISE)
            pay_out[:, b * inner : (b + 1) * inner] = tn(c_rows, (grown * dmix).astype(BF16)).astype(BF16)
        gn_out[...] = jnp.broadcast_to(gn_grad, (8, inner))

    return kernel


def scan_back_kernel(dims):
    batch, length, inner, heads, head_size, state = dims

    def kernel(
        dmix, prex, prebc, padx, padbc, step_in, cum_in, entered, returned, head_par,
        gpx_out, gpbc_out, dstep_out, headx_out, headbc_out, tapx_out, tapbc_out, heads_out,
        dx_buf,
    ):
        spread = spread_heads(inner, head_size)
        upper = (iota((length, length), 0) <= iota((length, length), 1)).astype(F32)
        causal = iota((length, length), 0) >= iota((length, length), 1)
        rate = -jnp.exp(head_par[1:2])
        skip = nn(head_par[...], spread, PRECISE)[2:3]
        lane = iota((length, LANES), 1)
        sub = iota((LANES, length), 0)
        tap_rows = [[None] * 5, [None] * 5]
        head_rows = [jnp.zeros((1, LANES), F32)] * 3
        for b in range(batch):
            rows = slice(b * length, (b + 1) * length)
            cols = slice(b * inner, (b + 1) * inner)
            dy = dmix[rows]
            px, pbc = prex[rows], prebc[rows]
            sgx, sgbc = sigmoid(px), sigmoid(pbc)
            x_act = (px * sgx).astype(BF16)
            bc = (pbc * sgbc).astype(BF16)
            b_rows, c_rows = bc[:, :state], bc[:, state:]
            x32 = x_act.astype(F32)
            step_raw, cum = step_in[rows], cum_in[rows]
            step = softplus(step_raw)
            total = cum[length - 1 : length]
            step_rep = nn(step, spread, PRECISE)
            grown = nn(jnp.exp(cum), spread, PRECISE)
            tail = nn(jnp.exp(total - cum), spread, PRECISE)
            step_x = step_rep * x32
            step_xb = step_x.astype(BF16)
            dyb = dy.astype(BF16)
            s_in, g_in = entered[:, cols], returned[:, cols]
            scores = nt(c_rows, b_rows)
            cum_t = cum.T
            dscores = jnp.zeros((length, length), F32)
            by_row = jnp.zeros((length, LANES), F32)
            by_col = jnp.zeros((LANES, length), F32)
            for h in range(heads):
                own = slice(h * head_size, (h + 1) * head_size)
                decay = jnp.exp(jnp.where(causal, cum[:, h : h + 1] - cum_t[h : h + 1, :], -1e30))
                dx_buf[:, own] = tn((scores * decay).astype(BF16), dyb[:, own])
                part = nt(dyb[:, own], step_xb[:, own]) * decay
                dscores = dscores + part
                part = part * scores
                by_row = jnp.where(lane == h, jnp.sum(part, 1, keepdims=True), by_row)
                by_col = jnp.where(sub == h, jnp.sum(part, 0, keepdims=True), by_col)
            dscores = dscores.astype(BF16)
            back = nn(b_rows, g_in)
            tail_back = tail * back
            dstep_x = dx_buf[...] + tail_back
            into = grown * nn(c_rows, s_in)
            leave = nt(step_x * tail_back, spread, PRECISE)
            dcum = by_row - by_col.T + nt(dy * into, spread, PRECISE) - leave
            held = jnp.sum(s_in.astype(F32) * g_in.astype(F32), 0, keepdims=True)
            held = nt(jnp.broadcast_to(held, (8, inner)), spread, PRECISE)[0:1] * jnp.exp(total)
            last = held + jnp.sum(leave, 0, keepdims=True)
            dlog = nn(upper, dcum, PRECISE) + last
            dstep = nt(dstep_x * x32, spread, PRECISE) + rate * dlog
            draw = dstep * sigmoid(step_raw)
            dstep_out[rows] = draw.astype(BF16)
            head_rows[0] = head_rows[0] + jnp.sum(draw, 0, keepdims=True)
            head_rows[1] = head_rows[1] + jnp.sum(dlog * (rate * step), 0, keepdims=True)
            dskip = jnp.sum(dy * x32, 0, keepdims=True)
            head_rows[2] = head_rows[2] + nt(jnp.broadcast_to(dskip, (8, inner)), spread, PRECISE)[0:1]
            db = tn(dscores, c_rows) + nt((tail * step_x).astype(BF16), g_in)
            dc = nn(dscores, b_rows) + nt((grown * dy).astype(BF16), s_in)
            dx = step_rep * dstep_x + skip * dy
            gpx = dx * sgx * (1.0 + px * (1.0 - sgx))
            slope = sgbc * (1.0 + pbc * (1.0 - sgbc))
            gpx_out[rows] = gpx
            gpbc_out[rows, :state] = db * slope[:, :state]
            gpbc_out[rows, state:] = dc * slope[:, state:]
            gpbc = gpbc_out[rows]
            headx_out[b * 8 : (b + 1) * 8] = gpx[0:8]
            headbc_out[b * 8 : (b + 1) * 8] = gpbc[0:8]
            base = b * (length + 8)
            for which, (gp, pad) in enumerate(((gpx, padx), (gpbc, padbc))):
                for k in range(5):
                    term = gp if k == 4 else gp * pad[base + 5 + k : base + 5 + k + length]
                    term = jnp.sum(term, 0, keepdims=True)
                    old = tap_rows[which][k]
                    tap_rows[which][k] = term if old is None else old + term
        for out, terms in ((tapx_out, tap_rows[0]), (tapbc_out, tap_rows[1])):
            out[...] = jnp.zeros_like(out)
            for k in range(5):
                out[k : k + 1] = terms[k]
        heads_out[...] = jnp.zeros_like(heads_out)
        for k in range(3):
            heads_out[k : k + 1] = head_rows[k]

    return kernel


def conv_back_kernel(dims):
    batch, length, inner, heads, head_size, state = dims

    def kernel(
        gpx, gpbc, aheadx, aheadbc, taps_x, taps_bc, dgate, dstep, w_gate, w_val, w_bc, w_dt,
        grx_out, grbc_out, part_out, extx, extbc,
    ):
        for b in range(batch):
            rows = slice(b * length, (b + 1) * length)
            part = nt(dgate[rows], w_gate[...]) + nt(dstep[rows], w_dt[...])
            for gp, ahead, taps, ext, weight, out in (
                (gpx, aheadx, taps_x, extx, w_val, grx_out),
                (gpbc, aheadbc, taps_bc, extbc, w_bc, grbc_out),
            ):
                ext[0:length] = gp[rows]
                ext[length : length + 8] = ahead[b * 8 : (b + 1) * 8]
                grad = taps[3:4] * ext[0:length]
                for k in range(3):
                    grad = grad + taps[k : k + 1] * ext[3 - k : 3 - k + length]
                grad = grad.astype(BF16)
                out[rows] = grad
                part = part + nt(grad, weight[...])
            part_out[rows] = part.astype(BF16)

    return kernel


def weight_kernel(normed, dgate, grx, grbc, dstep, normed_out, grad_out, zg_out, zv_out, bc_out, dt_out, wo_out):
    x = normed[...]
    zg_out[...] = tn(x, dgate[...]).astype(BF16)
    zv_out[...] = tn(x, grx[...]).astype(BF16)
    bc_out[...] = tn(x, grbc[...]).astype(BF16)
    dt_out[...] = tn(dstep[...], x)[: dt_out.shape[0]].astype(BF16)
    wo_out[...] = tn(normed_out[...], grad_out[...]).astype(BF16)


def norm_back_kernel(width):
    def kernel(place, parts, stream, residual, gain, grad_out, gain_out):
        total = parts[0].astype(F32)
        for p in range(1, parts.shape[0]):
            total = total + parts[p].astype(F32)
        x = stream[...].astype(F32)
        rstd = lax.rsqrt(jnp.mean(x * x, 1, keepdims=True) + EPSILON)
        gain_out[...] = jnp.broadcast_to(jnp.sum(total * x * rstd, 0, keepdims=True), gain_out.shape)
        weighted = total * gain[...]
        dot = jnp.sum(weighted * x, 1, keepdims=True)
        grad = rstd * weighted - x * (rstd * rstd * rstd * dot / width) + residual[...].astype(F32)
        grad_out[...] = grad.astype(BF16)

    return kernel


def shifted(shard, axis, by):
    peers = lax.axis_size(axis)
    pairs = [(i, i + by) for i in range(peers) if 0 <= i + by < peers]
    return lax.ppermute(shard, axis, pairs)


def gather_pieces(shard, axis):
    peers = lax.axis_size(axis)
    return [shard] + [
        lax.ppermute(shard, axis, [(i, i ^ s) for i in range(peers)]) for s in range(1, peers)
    ]


def swap(blocks, axis):
    return lax.all_to_all(blocks, axis, 0, 0)


def shards(
    hidden, cotangent, norm_gain, w_in_zx, w_in_dt, w_in_bc, conv_x, conv_x_bias, conv_bc,
    conv_bc_bias, dt_bias, a_log, d_skip, gate_norm, w_out,
):
    batch, length, width = hidden.shape
    rows = batch * length
    peers = lax.axis_size("head")
    ranks = lax.axis_size("seq")
    share = rows // peers
    layers, inner = w_out.shape[:2]
    heads = dt_bias.shape[1]
    head_size = inner // heads
    state = w_in_bc.shape[2] // 2
    inner_total = inner * peers
    dims = (batch, length, inner, heads, head_size, state)
    place = lax.axis_index("head").astype(jnp.int32).reshape(1)

    hidden_rows = hidden.reshape(rows, width)
    cot_rows = cotangent.reshape(rows, width)
    w_zx = jnp.transpose(w_in_zx, (0, 2, 1, 3))
    w_dt = jnp.pad(w_in_dt, ((0, 0), (0, 0), (0, LANES - heads)))
    head_par = jnp.pad(jnp.stack([dt_bias, a_log, d_skip], 1), ((0, 0), (0, 5), (0, LANES - heads)))
    taps_x = jnp.pad(jnp.concatenate([conv_x, conv_x_bias[:, None]], 1), ((0, 0), (0, 3), (0, 0)))
    taps_bc = jnp.pad(jnp.concatenate([conv_bc, conv_bc_bias[:, None]], 1), ((0, 0), (0, 3), (0, 0)))
    gates = gate_norm[:, None]
    gains = norm_gain[:, None]

    def norm_low(x, gain):
        x = x.astype(F32)
        return (x * lax.rsqrt(jnp.mean(x * x, -1, keepdims=True) + EPSILON) * gain).astype(BF16)

    hidden_halo = shifted(hidden[:, length - HALO :], "seq", 1)
    gate_pieces = gather_pieces(jnp.broadcast_to(gates, (layers, 8, inner)), "head")
    out_pieces = [gather_pieces(w_out[0], "head"), None]
    normed = norm_low(hidden_rows, norm_gain[0])
    halo = norm_low(hidden_halo, norm_gain[0]).reshape(batch * HALO, width)
    stream = hidden_rows
    saved = []
    for l in range(layers):
        last = l == layers - 1
        sub = lambda a, extra=None: layer_spec(a, l, extra)
        pad = batch * (length + 8)
        gate, padx, padbc, prex, prebc, local, step, cum, pay = call(
            forward_kernel(dims),
            [
                ((rows, inner), F32), ((pad, inner), F32), ((pad, 2 * state), F32),
                ((rows, inner), F32), ((rows, 2 * state), F32), ((rows, inner), F32),
                ((rows, LANES), F32), ((rows, LANES), F32), ((state, batch * inner + LANES), BF16),
            ],
            [normed, halo, w_zx, w_zx, w_in_bc, w_dt, taps_x, taps_bc, head_par],
            [None, None, sub(w_zx, 0), sub(w_zx, 1), sub(w_in_bc), sub(w_dt), sub(taps_x), sub(taps_bc),
             sub(head_par)],
            [pltpu.VMEM((length, inner), F32)],
        )
        parts = swap(pay.reshape(ranks, state // ranks, batch * inner + LANES), "seq")
        entered = call(
            scan_kernel(head_size, False),
            [((ranks, state // ranks, batch * inner), BF16)],
            [parts, parts],
        )[0]
        entered = swap(entered, "seq").reshape(state, batch * inner)
        kept = dict(
            normed=normed, stream=stream, gate=gate, padx=padx, padbc=padbc, prex=prex, prebc=prebc,
            step=step, cum=cum, parts=parts, entered=entered,
        )
        args = [local, gate, prebc, cum, entered, gates]
        specs = [None] * 5 + [sub(gates)]
        outs = [((rows, inner), F32), ((rows, inner), BF16)]
        if last:
            args += [cot_rows, w_out]
            specs += [None, sub(w_out)]
            outs += [((8, length), F32)]
        mixed, q, *sums = call(mix_kernel(dims, last), outs, args, specs)
        kept["mixed"] = mixed
        if last:
            kept["sources"] = gather_pieces(sums[0], "head")
        qs = gather_pieces(q, "head")
        outs = [((rows, width), F32)]
        if not last:
            outs += [((rows, width), BF16), ((rows, width), F32), ((rows, LANES), F32)]
        gain_next = min(l + 1, layers - 1)
        piece_specs = [layer_spec(g[:, :1], l) for g in gate_pieces]
        after = call(
            out_kernel(dims, peers, inner_total, last),
            outs,
            [stream, gains, *qs, *out_pieces[l], *[g[:, :1] for g in gate_pieces]],
            [None, layer_spec(gains, gain_next)] + [None] * (2 * peers) + piece_specs,
        )
        if last:
            final_out = after[0]
        else:
            stream, normed, u, rstd = after
            kept["sources"] = [u, rstd]
            halo = shifted(normed.reshape(batch, length, width)[:, length - HALO :], "seq", 1)
            halo = halo.reshape(batch * HALO, width)
            held, normed = lax.optimization_barrier((w_out[l + 1], normed))
            out_pieces[l + 1] = gather_pieces(held, "head")
        saved.append(kept)

    grad = cot_rows
    done = [None] * layers
    gain_rows = [None] * layers
    for l in range(layers - 1, -1, -1):
        last = l == layers - 1
        sub = lambda a, extra=None: layer_spec(a, l, extra)
        kept = saved[l]
        sources = kept["sources"]
        dmix, dgate, kept_out, pay, gn_grad = call(
            gate_back_kernel(dims, inner_total, last, peers),
            [((rows, inner), F32), ((rows, inner), BF16), ((rows, inner), BF16),
             ((state, batch * inner), BF16), ((8, inner), F32)],
            [grad, w_out, kept["mixed"], kept["gate"], kept["prebc"], kept["cum"], gates, *sources],
            [None, sub(w_out), None, None, None, None, sub(gates)] + [None] * len(sources),
        )
        back = swap(pay.reshape(ranks, state // ranks, batch * inner), "seq")
        returned = call(
            scan_kernel(head_size, True),
            [((ranks, state // ranks, batch * inner), BF16)],
            [back, kept["parts"]],
        )[0]
        returned = swap(returned, "seq").reshape(state, batch * inner)
        gpx, gpbc, dstep, headx, headbc, tapx, tapbc, head_grads = call(
            scan_back_kernel(dims),
            [((rows, inner), F32), ((rows, 2 * state), F32), ((rows, LANES), BF16),
             ((batch * 8, inner), F32), ((batch * 8, 2 * state), F32),
             ((8, inner), F32), ((8, 2 * state), F32), ((8, LANES), F32)],
            [dmix, kept["prex"], kept["prebc"], kept["padx"], kept["padbc"], kept["step"], kept["cum"],
             kept["entered"], returned, head_par],
            [None] * 9 + [sub(head_par)],
            [pltpu.VMEM((length, inner), F32)],
        )
        aheadx = shifted(headx, "seq", -1)
        aheadbc = shifted(headbc, "seq", -1)
        grx, grbc, part = call(
            conv_back_kernel(dims),
            [((rows, inner), BF16), ((rows, 2 * state), BF16), ((rows, width), BF16)],
            [gpx, gpbc, aheadx, aheadbc, taps_x, taps_bc, dgate, dstep, w_zx, w_zx, w_in_bc, w_dt],
            [None] * 4 + [sub(taps_x), sub(taps_bc), None, None, sub(w_zx, 0), sub(w_zx, 1), sub(w_in_bc),
                          sub(w_dt)],
            [pltpu.VMEM((length + 8, inner), F32), pltpu.VMEM((length + 8, 2 * state), F32)],
        )
        grad_in = grad
        parts = swap(part.reshape(peers, share, width), "head")
        grad_share, gain_grad = call(
            norm_back_kernel(width),
            [((share, width), BF16), ((8, width), F32)],
            [parts, kept["stream"], grad, gains],
            [None] + [pl.BlockSpec((share, width), lambda _, at: (at[0], 0))] * 2 + [sub(gains)],
            prefetch=place,
        )
        grad = lax.all_gather(grad_share, "head", axis=0, tiled=True)
        gain_rows[l] = gain_grad[0]
        head_rows = -(-heads // 8) * 8
        zg, zv, bc, dt, wo = call(
            weight_kernel,
            [((width, inner), BF16), ((width, inner), BF16), ((width, 2 * state), BF16),
             ((head_rows, width), BF16), ((inner, width), BF16)],
            [kept["normed"], dgate, grx, grbc, dstep, kept_out, grad_in],
        )
        bc_total = width + 8
        bc_rows = -(-bc_total // (16 * peers)) * 16 * peers
        packed = jnp.concatenate(
            [bc, tapbc.astype(BF16), jnp.zeros((bc_rows - bc_total, 2 * state), BF16)], 0
        )
        packed = swap(packed.reshape(peers, bc_rows // peers, 2 * state), "head")
        packed = jnp.sum(packed.astype(F32), 0).astype(BF16)
        small = jnp.concatenate([tapx, gn_grad, jnp.pad(head_grads, ((0, 0), (0, width - LANES)))[:, :inner]], 0)
        zg, zv, wo, dt, packed, small = lax.psum((zg, zv, wo, dt, packed, small.astype(BF16)), "seq")
        packed = lax.all_gather(packed, "head", axis=0, tiled=True).astype(F32)
        small = small.astype(F32)
        done[l] = dict(
            zx=jnp.stack([zg, zv], 1).astype(F32),
            dt=dt[:heads].T.astype(F32),
            bc=packed[:width],
            conv_x=small[:4],
            conv_x_bias=small[4],
            conv_bc=packed[width : width + 4],
            conv_bc_bias=packed[width + 4],
            dt_bias=small[16, :heads],
            a_log=small[17, :heads],
            d_skip=small[18, :heads],
            gate_norm=small[8],
            wo=wo.astype(F32),
        )
    gain_sum = sum(gather_pieces(jnp.stack(gain_rows), "head"))
    hop = 1
    while hop < ranks:
        gain_sum = gain_sum + lax.ppermute(gain_sum, "seq", [(i, i ^ hop) for i in range(ranks)])
        hop *= 2
    both = lambda name: jnp.stack([d[name] for d in done])
    return (
        final_out.reshape(hidden.shape),
        grad.astype(F32).reshape(hidden.shape),
        gain_sum,
        both("zx"),
        both("dt"),
        both("bc"),
        both("conv_x"),
        both("conv_x_bias"),
        both("conv_bc"),
        both("conv_bc_bias"),
        both("dt_bias"),
        both("a_log"),
        both("d_skip"),
        both("gate_norm"),
        both("wo"),
    )


def solution(mesh):
    tokens = P(None, "seq", None)
    heads = P(None, "head")
    last = P(None, None, "head")
    placed = (
        tokens, tokens, P(), P(None, None, None, "head"), last, P(), last, heads, P(), P(), heads, heads,
        heads, heads, P(None, "head", None),
    )
    results = (
        tokens, tokens, P(), P(None, None, None, "head"), last, P(), last, heads, P(), P(), heads, heads,
        heads, heads, P(None, "head", None),
    )
    return jax.shard_map(shards, mesh=mesh, in_specs=placed, out_specs=results, check_vma=False)
```

time: 888 us -> 623 us (0.70)
  other arithmetic: 162 us -> 17.5 us
  waiting for transfers between devices: 332 us -> 220 us
  matrix products: 103 us -> 0 us
  Pallas kernels: 0 us -> 99.5 us
  starting transfers between devices: 7.72 us -> 78.6 us
  local copies, waits for them, and re-layouts: 94.5 us -> 24.1 us
    ppermute x0 -> x24, waiting for transfers between devices: none -> 144 us  [the longest x21 143 us: gather_pieces(): lax.ppermute(shard, axis, [(i, i ^ s) for i in range(peers)])]
    reduce_scatter x4 -> x0, waiting for transfers between devices: 130 us -> none  [the longest x2 73.7 us: shards(): lax.psum_scatter(jnp.dot(normed_rows, out_weight, preferred_element_type=...]
    dot_general x54 -> x0, matrix products: 103 us -> none  [the longest x6 31 us: span_step(): outputs = jnp.einsum('btsh,bshp->bthp', mixing, inputs, precision=PRECISE)]
    pallas_call x0 -> x20, Pallas kernels: none -> 99.5 us  [call(): pl.pallas_call(kernel, grid_spec=pltpu.PrefetchScalarGridSpec(num_scalar_...]
    all_gather x6 -> x0, waiting for transfers between devices: 94 us -> none  [the longest x4 59.3 us: entering(): gathered = jax.tree.map(lambda a: lax.all_gather(a, axis), part)]
    psum x3 -> x1, waiting for transfers between devices: 106 us -> 26.5 us  [shards(): lax.psum((zg, zv, wo, dt, packed, small.astype(BF16)), 'seq')]
    another operation x36 -> x20, other arithmetic: 84.5 us -> 8.47 us  [the longest x12 7.82 us: shards(): both = lambda name: jnp.stack([d[name] for d in done])]
    all_to_all x0 -> x6, blocking collectives: none -> 65.9 us  [swap(): return lax.all_to_all(blocks, axis, 0, 0)]
  transfers between devices with their start and end apart: 17 -> 37, of which waited for: 14 -> 20; matrix products, arithmetic and copies ran while one was open for 18% -> 3% of each run, Pallas kernels for 0% -> 4%
where the time goes in v1:
time: 623 us; the launch traced here: 613 us
  waiting for transfers between devices  220 us (35%)
  blocking collectives  158 us (25%)
  Pallas kernels  99.5 us (16%)
  starting transfers between devices  78.6 us (13%)
  local copies, waits for them, and re-layouts  24.1 us (4%)
  other arithmetic  17.5 us (3%)
  between operations  15 us (2%)
    ppermute x21, waiting for transfers between devices, gather_pieces(): lax.ppermute(shard, axis, [(i, i ^ s) for i in range(peers)])  143 us
    pallas_call x20, Pallas kernels, call(): pl.pallas_call(kernel, grid_spec=pltpu.PrefetchScalarGridSpec(num_scalar_...  99.5 us
    all_to_all x6, blocking collectives, swap(): return lax.all_to_all(blocks, axis, 0, 0)  65.9 us
    all_to_all x6, waiting for transfers between devices, swap(): return lax.all_to_all(blocks, axis, 0, 0)  46.8 us
    ppermute x21, starting transfers between devices, gather_pieces(): lax.ppermute(shard, axis, [(i, i ^ s) for i in range(peers)])  37.2 us
    all_gather x2, blocking collectives, shards(): grad = lax.all_gather(grad_share, 'head', axis=0, tiled=True)  36.7 us
    all_gather x2, blocking collectives, shards(): packed = lax.all_gather(packed, 'head', axis=0, tiled=True).astype(F32)  30.8 us
    all_to_all x6, starting transfers between devices, swap(): return lax.all_to_all(blocks, axis, 0, 0)  28 us
  transfers between devices with their start and end apart: 37, of which 20 were waited for; matrix products, arithmetic and copies ran while one was open for 3% of the time, Pallas kernels for 4%

profile of v1, /device:TPU:0, one launch (start us, length us, event | category | flops | bytes accessed | tf_op | source)
XLA Modules:
  0.0 612.5 jit_solution(10742348152881655183)
XLA Ops:
  49.5 13.7 %collective-permute-done.7 = f32[2,8,384]{2,1,0:T(8,128)S(1)} collective-permute-done((f32[2,8,384]{2,1,0:T(8,128)S(1)}, f32[2,8,384]{2,1,0:T(8,128)S(1)}, u32[]{:S(2)}, u32[]{:S(2)}) %collective-permute-start.7) | collective-permute-done | bytes 24608 | tf_op jit(solution)/shard_map/ppermute | solution.py:433
  68.3 21.9 %collective-permute-done.8 = f32[2,8,384]{2,1,0:T(8,128)S(1)} collective-permute-done((f32[2,8,384]{2,1,0:T(8,128)S(1)}, f32[2,8,384]{2,1,0:T(8,128)S(1)}, u32[]{:S(2)}, u32[]{:S(2)}) %collective-permute-start.8) | collective-permute-done | bytes 24608 | tf_op jit(solution)/shard_map/ppermute | solution.py:433
  97.1 12.4 %collective-permute-done.1.rest_1_ = bf16[512,384]{1,0:T(8,128)(2,1)S(1)} collective-permute-done((bf16[512,384]{1,0:T(8,128)(2,1)}, bf16[512,384]{1,0:T(8,128)(2,1)S(1)}, u32[]{:S(2)}, u32[]{:S(2)}) %collective-permute-start.1) | collective-permute-done | bytes 393248 | tf_op jit(solution)/shard_map/ppermute | solution.py:433
  109.5 11.1 %collective-permute-done.2.rest_2_ = bf16[512,384]{1,0:T(8,128)(2,1)} collective-permute-done((bf16[512,384]{1,0:T(8,128)(2,1)}, bf16[512,384]{1,0:T(8,128)(2,1)}, u32[]{:S(2)}, u32[]{:S(2)}) %collective-permute-start.2) | collective-permute-done | bytes 393248 | tf_op jit(solution)/shard_map/ppermute | solution.py:433
  138.9 13.9 %all_to_all.60.part.decays = bf16[8,16,896]{2,1,0:T(8,128)(2,1)} all-to-all(bf16[8,16,896]{2,1,0:T(8,128)(2,1)} %bitcast.98), channel_id=1, replica_groups=mesh['seq'=8,'head'=4] {'seq'}, dimensions={0} | all-to-all | bytes 458752 | tf_op jit(solution)/shard_map/all_to_all | solution.py:438
  154.8 10.2 %all_to_all.61 = bf16[8,16,768]{2,1,0:T(8,128)(2,1)} all-to-all(bf16[8,16,768]{2,1,0:T(8,128)(2,1)} %shard_map.267), channel_id=1, replica_groups=mesh['seq'=8,'head'=4] {'seq'}, dimensions={0} | all-to-all | bytes 393216 | tf_op jit(solution)/shard_map/all_to_all | solution.py:438
  189.7 10.2 %all_to_all.62.part = bf16[8,16,768]{2,1,0:T(8,128)(2,1)} all-to-all(bf16[8,16,768]{2,1,0:T(8,128)(2,1)} %bitcast.100), channel_id=1, replica_groups=mesh['seq'=8,'head'=4] {'seq'}, dimensions={0} | all-to-all | bytes 393216 | tf_op jit(solution)/shard_map/all_to_all | solution.py:438
  201.9 10.4 %all_to_all.63 = bf16[8,16,768]{2,1,0:T(8,128)(2,1)} all-to-all(bf16[8,16,768]{2,1,0:T(8,128)(2,1)} %shard_map.271), channel_id=1, replica_groups=mesh['seq'=8,'head'=4] {'seq'}, dimensions={0} | all-to-all | bytes 393216 | tf_op jit(solution)/shard_map/all_to_all | solution.py:438
  212.3 10.7 %shard_map.272 = (f32[512,384]{1,0:T(8,128)}, f32[512,256]{1,0:T(8,128)}, bf16[512,128]{1,0:T(8,128)(2,1)}, f32[16,384]{1,0:T(8,128)}, f32[16,256]{1,0:T(8,128)}...) custom-call(f32[512,384]{1,0:T(8,128)} %get-tuple-element.108.dmix, f32[512,384]{1,0:T(8,128)} %get-tuple-element.109.prex, ...), custom_call_target="tpu_custom_call" | custom-call | tf_op jit(solution)/shard_map/pallas_call | solution.py:62
  237.0 20.5 %all-to-all-done.6.parts = bf16[4,128,768]{2,1,0:T(8,128)(2,1)S(1)} async-done(((bf16[4,128,768]{2,1,0:T(8,128)(2,1)}), bf16[4,128,768]{2,1,0:T(8,128)(2,1)S(1)}, u32[]{:S(2)}, u32[]{:S(2)}) %all-to-all-start.6) | async-done | bytes 786464 | tf_op jit(solution)/shard_map/all_to_all | solution.py:438
  260.5 18.9 %all_gather.12.grad_out.residual = bf16[512,768]{1,0:T(8,128)(2,1)} all-gather(bf16[128,768]{1,0:T(8,128)(2,1)} %get-tuple-element.121), channel_id=1, replica_groups=mesh['seq'=8,'head'=4] {'head'}, dimensions={0}, use_global_device_ids=true | all-gather | bytes 983040 | tf_op jit(solution)/shard_map/all_gather | solution.py:591
  284.6 11.0 %all_to_all.64.part = bf16[8,16,768]{2,1,0:T(8,128)(2,1)} all-to-all(bf16[8,16,768]{2,1,0:T(8,128)(2,1)} %bitcast.101), channel_id=1, replica_groups=mesh['seq'=8,'head'=4] {'seq'}, dimensions={0} | all-to-all | bytes 393216 | tf_op jit(solution)/shard_map/all_to_all | solution.py:438
  297.6 10.2 %all_to_all.65 = bf16[8,16,768]{2,1,0:T(8,128)(2,1)} all-to-all(bf16[8,16,768]{2,1,0:T(8,128)(2,1)} %shard_map.276), channel_id=1, replica_groups=mesh['seq'=8,'head'=4] {'seq'}, dimensions={0} | all-to-all | bytes 393216 | tf_op jit(solution)/shard_map/all_to_all | solution.py:438
  307.8 10.7 %shard_map.277 = (f32[512,384]{1,0:T(8,128)}, f32[512,256]{1,0:T(8,128)}, bf16[512,128]{1,0:T(8,128)(2,1)}, f32[16,384]{1,0:T(8,128)}, f32[16,256]{1,0:T(8,128)}...) custom-call(f32[512,384]{1,0:T(8,128)} %get-tuple-element.125.dmix, f32[512,384]{1,0:T(8,128)} %get-tuple-element.126.prex, ...), custom_call_target="tpu_custom_call" | custom-call | tf_op jit(solution)/shard_map/pallas_call | solution.py:62
  361.4 13.2 %collective-permute-done.14.rest_5_ = bf16[384,768]{1,0:T(8,128)(2,1)S(1)} collective-permute-done((bf16[384,768]{1,0:T(8,128)(2,1)S(1)}, bf16[384,768]{1,0:T(8,128)(2,1)S(1)}, u32[]{:S(2)}, u32[]{:S(2)}) %collective-permute-start.14) | collective-permute-done | bytes 589856 | tf_op jit(solution)/shard_map/ppermute | solution.py:433
  375.8 18.1 %collective-permute-done.15.rest_6_ = bf16[384,768]{1,0:T(8,128)(2,1)S(1)} collective-permute-done((bf16[384,768]{1,0:T(8,128)(2,1)S(1)}, bf16[384,768]{1,0:T(8,128)(2,1)S(1)}, u32[]{:S(2)}, u32[]{:S(2)}) %collective-permute-start.15) | collective-permute-done | bytes 589856 | tf_op jit(solution)/shard_map/ppermute | solution.py:433
  401.6 37.3 %collective-permute-done.12.rest_2_ = bf16[512,384]{1,0:T(8,128)(2,1)} collective-permute-done((bf16[512,384]{1,0:T(8,128)(2,1)}, bf16[512,384]{1,0:T(8,128)(2,1)}, u32[]{:S(2)}, u32[]{:S(2)}) %collective-permute-start.12) | collective-permute-done | bytes 393248 | tf_op jit(solution)/shard_map/ppermute | solution.py:433
  445.4 24.1 %all-reduce.6 = (bf16[8,768]{1,0:T(8,128)(2,1)S(1)}, bf16[8,768]{1,0:T(8,128)(2,1)S(1)}, bf16[24,384]{1,0:T(8,128)(2,1)S(1)}, bf16[24,384]{1,0:T(8,128)(2,1)S(1)}) all-reduce(bf16[8,768]{1,0:T(8,128)(2,1)S(1)} %copy-done.36, bf16[8,768]{1,0:T(8,128)(2,1)S(1)} %copy-done.37, ...), channel_id=1, replica_groups=mesh['seq'=8,'head'=4] {'seq'}, use_global_device_ids=true, to_apply=%region_7.8 | all-reduce | flops 30720 | bytes 122880 | tf_op jit(solution)/shard_map/psum | solution.py:608
  469.5 10.3 %all-to-all-start.9 = ((bf16[4,128,768]{2,1,0:T(8,128)(2,1)}), bf16[4,128,768]{2,1,0:T(8,128)(2,1)S(1)}, u32[]{:S(2)}, u32[]{:S(2)}) async-start(bf16[4,128,768]{2,1,0:T(8,128)(2,1)} %bitcast.25), calls=%async_computation.9 | async-start | bytes 1572864 | tf_op jit(solution)/shard_map/all_to_all | solution.py:438
  483.1 14.3 %all-to-all-done.9.parts = bf16[4,128,768]{2,1,0:T(8,128)(2,1)S(1)} async-done(((bf16[4,128,768]{2,1,0:T(8,128)(2,1)}), bf16[4,128,768]{2,1,0:T(8,128)(2,1)S(1)}, u32[]{:S(2)}, u32[]{:S(2)}) %all-to-all-start.9) | async-done | bytes 786464 | tf_op jit(solution)/shard_map/all_to_all | solution.py:438
  516.4 17.9 %all_gather.13 = bf16[512,768]{1,0:T(8,128)(2,1)S(1)} all-gather(bf16[128,768]{1,0:T(8,128)(2,1)} %get-tuple-element.138), channel_id=1, replica_groups=mesh['seq'=8,'head'=4] {'head'}, dimensions={0}, use_global_device_ids=true | all-gather | bytes 983040 | tf_op jit(solution)/shard_map/all_gather | solution.py:591
  536.1 26.5 %all-reduce.10.cloned.1.call-done = (bf16[1,768,1,384]{3,1,2,0:T(8,128)(2,1)}, bf16[1,768,1,384]{3,1,2,0:T(8,128)(2,1)}, bf16[1,768,1,384]{3,1,2,0:T(8,128)(2,1)...) async-done(((bf16[1,768,1,384]{3,1,2,0:T(8,128)(2,1)}, ...) | async-done | bytes 3751952 | tf_op jit(solution)/shard_map/psum | solution.py:608
  562.7 15.1 %all_gather.15 = bf16[832,256]{1,0:T(8,128)(2,1)S(1)} all-gather(bf16[208,256]{1,0:T(8,128)(2,1)} %get-tuple-element.188), channel_id=1, replica_groups=mesh['seq'=8,'head'=4] {'head'}, dimensions={0}, use_global_device_ids=true | all-gather | bytes 532480 | tf_op jit(solution)/shard_map/all_gather | solution.py:609
  577.9 15.7 %all_gather.14 = bf16[832,256]{1,0:T(8,128)(2,1)S(1)} all-gather(bf16[208,256]{1,0:T(8,128)(2,1)S(1)} %copy-done.22), channel_id=1, replica_groups=mesh['seq'=8,'head'=4] {'head'}, dimensions={0}, use_global_device_ids=true | all-gather | bytes 532480 | tf_op jit(solution)/shard_map/all_gather | solution.py:609
  (262 shorter events, 219.0 us)
Async XLA Ops:
  8.1 12.6 %collective-permute-start = (bf16[2,16,768]{2,1,0:T(8,128)(2,1)S(1)}, bf16[2,16,768]{2,1,0:T(8,128)(2,1)S(1)}, u32[]{:S(2)}, u32[]{:S(2)}) collective-permute-start(bf16[2,16,768]{2,1,0:T(8,128)(2,1)S(1)} %slice.105), channel_id=1, source_target_pairs={{0,4},{4,8},{8,12},{12,16},{16,20},{20,24},{24,28},{1,5},{5,9},{9,... | collective-permute-start | bytes 147464 | tf_op jit(solution)/shard_map/ppermute | solution.py:427
  12.0 81.3 %collective-permute-start.4 = (bf16[384,768]{1,0:T(8,128)(2,1)S(1)}, bf16[384,768]{1,0:T(8,128)(2,1)S(1)}, u32[]{:S(2)}, u32[]{:S(2)}) collective-permute-start(bf16[384,768]{1,0:T(8,128)(2,1)S(1)} %get-tuple-element.193.rest_4_), channel_id=1, source_target_pairs={{0,1},{1,0},{2,3},{3,2},{4,5},{5,4},{6,7},{7,6},{8,9},{9,8},{10,11... | collective-permute-start | bytes 1769480 | tf_op jit(solution)/shard_map/ppermute | solution.py:433
  29.9 10.5 %all-to-all-start = ((bf16[8,16,896]{2,1,0:T(8,128)(2,1)}), bf16[8,16,896]{2,1,0:T(8,128)(2,1)S(1)}, u32[]{:S(2)}, u32[]{:S(2)}) async-start(bf16[8,16,896]{2,1,0:T(8,128)(2,1)} %bitcast.97), calls=%async_computation | async-start | bytes 458752 | tf_op jit(solution)/shard_map/all_to_all | solution.py:438
  33.8 63.2 %collective-permute-start.5 = (bf16[384,768]{1,0:T(8,128)(2,1)S(1)}, bf16[384,768]{1,0:T(8,128)(2,1)S(1)}, u32[]{:S(2)}, u32[]{:S(2)}) collective-permute-start(bf16[384,768]{1,0:T(8,128)(2,1)S(1)} %get-tuple-element.193.rest_4_), channel_id=1, source_target_pairs={{0,2},{1,3},{2,0},{3,1},{4,6},{5,7},{6,4},{7,5},{8,10},{9,11},{10,... | collective-permute-start | bytes 1769480 | tf_op jit(solution)/shard_map/ppermute | solution.py:433
  36.4 60.7 %collective-permute-start.6 = (bf16[384,768]{1,0:T(8,128)(2,1)S(1)}, bf16[384,768]{1,0:T(8,128)(2,1)S(1)}, u32[]{:S(2)}, u32[]{:S(2)}) collective-permute-start(bf16[384,768]{1,0:T(8,128)(2,1)S(1)} %get-tuple-element.193.rest_4_), channel_id=1, source_target_pairs={{0,3},{1,2},{2,1},{3,0},{4,7},{5,6},{6,5},{7,4},{8,11},{9,10},{10,... | collective-permute-start | bytes 1769480 | tf_op jit(solution)/shard_map/ppermute | solution.py:433
  43.0 21.1 %all-to-all-start.1 = ((bf16[8,16,768]{2,1,0:T(8,128)(2,1)}), bf16[8,16,768]{2,1,0:T(8,128)(2,1)S(1)}, u32[]{:S(2)}, u32[]{:S(2)}) async-start(bf16[8,16,768]{2,1,0:T(8,128)(2,1)} %shard_map.263), calls=%async_computation.1 | async-start | bytes 393216 | tf_op jit(solution)/shard_map/all_to_all | solution.py:438
  46.4 16.8 %collective-permute-start.7 = (f32[2,8,384]{2,1,0:T(8,128)S(1)}, f32[2,8,384]{2,1,0:T(8,128)S(1)}, u32[]{:S(2)}, u32[]{:S(2)}) collective-permute-start(f32[2,8,384]{2,1,0:T(8,128)S(1)} %broadcast_in_dim.23), channel_id=1, source_target_pairs={{0,1},{1,0},{2,3},{3,2},{4,5},{5,4},{6,7},{7,6},{8,9},{9,8},{10,11... | collective-permute-start | bytes 73736 | tf_op jit(solution)/shard_map/ppermute | solution.py:433
  46.9 43.3 %collective-permute-start.8 = (f32[2,8,384]{2,1,0:T(8,128)S(1)}, f32[2,8,384]{2,1,0:T(8,128)S(1)}, u32[]{:S(2)}, u32[]{:S(2)}) collective-permute-start(f32[2,8,384]{2,1,0:T(8,128)S(1)} %broadcast_in_dim.23), channel_id=1, source_target_pairs={{0,2},{1,3},{2,0},{3,1},{4,6},{5,7},{6,4},{7,5},{8,10},{9,11},{10,... | collective-permute-start | bytes 73736 | tf_op jit(solution)/shard_map/ppermute | solution.py:433
  63.3 27.0 %collective-permute-start.9 = (f32[2,8,384]{2,1,0:T(8,128)S(1)}, f32[2,8,384]{2,1,0:T(8,128)S(1)}, u32[]{:S(2)}, u32[]{:S(2)}) collective-permute-start(f32[2,8,384]{2,1,0:T(8,128)S(1)} %broadcast_in_dim.23), channel_id=1, source_target_pairs={{0,3},{1,2},{2,1},{3,0},{4,7},{5,6},{6,5},{7,4},{8,11},{9,10},{10,... | collective-permute-start | bytes 73736 | tf_op jit(solution)/shard_map/ppermute | solution.py:433
  90.3 19.2 %collective-permute-start.1 = (bf16[512,384]{1,0:T(8,128)(2,1)}, bf16[512,384]{1,0:T(8,128)(2,1)S(1)}, u32[]{:S(2)}, u32[]{:S(2)}) collective-permute-start(bf16[512,384]{1,0:T(8,128)(2,1)} %get-tuple-element.95.rest_0_), channel_id=1, source_target_pairs={{0,1},{1,0},{2,3},{3,2},{4,5},{5,4},{6,7},{7,6},{8,9},{9,8},{10,11... | collective-permute-start | bytes 1179656 | tf_op jit(solution)/shard_map/ppermute | solution.py:433
  90.3 30.3 %collective-permute-start.2 = (bf16[512,384]{1,0:T(8,128)(2,1)}, bf16[512,384]{1,0:T(8,128)(2,1)}, u32[]{:S(2)}, u32[]{:S(2)}) collective-permute-start(bf16[512,384]{1,0:T(8,128)(2,1)} %get-tuple-element.95.rest_0_), channel_id=1, source_target_pairs={{0,2},{1,3},{2,0},{3,1},{4,6},{5,7},{6,4},{7,5},{8,10},{9,11},{10,... | collective-permute-start | bytes 1179656 | tf_op jit(solution)/shard_map/ppermute | solution.py:433
  93.4 27.2 %collective-permute-start.3 = (bf16[512,384]{1,0:T(8,128)(2,1)}, bf16[512,384]{1,0:T(8,128)(2,1)}, u32[]{:S(2)}, u32[]{:S(2)}) collective-permute-start(bf16[512,384]{1,0:T(8,128)(2,1)} %get-tuple-element.95.rest_0_), channel_id=1, source_target_pairs={{0,3},{1,2},{2,1},{3,0},{4,7},{5,6},{6,5},{7,4},{8,11},{9,10},{10,... | collective-permute-start | bytes 1179656 | tf_op jit(solution)/shard_map/ppermute | solution.py:433
  233.5 24.0 %all-to-all-start.6 = ((bf16[4,128,768]{2,1,0:T(8,128)(2,1)}), bf16[4,128,768]{2,1,0:T(8,128)(2,1)S(1)}, u32[]{:S(2)}, u32[]{:S(2)}) async-start(bf16[4,128,768]{2,1,0:T(8,128)(2,1)} %bitcast.90), calls=%async_computation.6 | async-start | bytes 1572864 | tf_op jit(solution)/shard_map/all_to_all | solution.py:438
  337.4 16.2 %all-to-all-start.10 = ((bf16[4,208,256]{2,1,0:T(8,128)(2,1)}), bf16[4,208,256]{2,1,0:T(8,128)(2,1)S(1)}, u32[]{:S(2)}, u32[]{:S(2)}) async-start(bf16[4,208,256]{2,1,0:T(8,128)(2,1)} %bitcast.35), calls=%async_computation.10 | async-start | bytes 851968 | tf_op jit(solution)/shard_map/all_to_all | solution.py:438
  340.8 33.8 %collective-permute-start.14 = (bf16[384,768]{1,0:T(8,128)(2,1)S(1)}, bf16[384,768]{1,0:T(8,128)(2,1)S(1)}, u32[]{:S(2)}, u32[]{:S(2)}) collective-permute-start(bf16[384,768]{1,0:T(8,128)(2,1)S(1)} %get-tuple-element.105.rest_4_), channel_id=1, source_target_pairs={{0,1},{1,0},{2,3},{3,2},{4,5},{5,4},{6,7},{7,6},{8,9},{9,8},{10,11... | collective-permute-start | bytes 1769480 | tf_op jit(solution)/shard_map/ppermute | solution.py:433
  342.8 51.1 %collective-permute-start.15 = (bf16[384,768]{1,0:T(8,128)(2,1)S(1)}, bf16[384,768]{1,0:T(8,128)(2,1)S(1)}, u32[]{:S(2)}, u32[]{:S(2)}) collective-permute-start(bf16[384,768]{1,0:T(8,128)(2,1)S(1)} %get-tuple-element.105.rest_4_), channel_id=1, source_target_pairs={{0,2},{1,3},{2,0},{3,1},{4,6},{5,7},{6,4},{7,5},{8,10},{9,11},{10,... | collective-permute-start | bytes 1769480 | tf_op jit(solution)/shard_map/ppermute | solution.py:433
  345.2 48.7 %collective-permute-start.16 = (bf16[384,768]{1,0:T(8,128)(2,1)S(1)}, bf16[384,768]{1,0:T(8,128)(2,1)S(1)}, u32[]{:S(2)}, u32[]{:S(2)}) collective-permute-start(bf16[384,768]{1,0:T(8,128)(2,1)S(1)} %get-tuple-element.105.rest_4_), channel_id=1, source_target_pairs={{0,3},{1,2},{2,1},{3,0},{4,7},{5,6},{6,5},{7,4},{8,11},{9,10},{10,... | collective-permute-start | bytes 1769480 | tf_op jit(solution)/shard_map/ppermute | solution.py:433
  353.6 116.0 %all-to-all-start.11 = ((bf16[4,208,256]{2,1,0:T(8,128)(2,1)}), bf16[4,208,256]{2,1,0:T(8,128)(2,1)S(1)}, u32[]{:S(2)}, u32[]{:S(2)}) async-start(bf16[4,208,256]{2,1,0:T(8,128)(2,1)} %bitcast.37), calls=%async_computation.11 | async-start | bytes 851968 | tf_op jit(solution)/shard_map/all_to_all | solution.py:438
  357.0 44.6 %collective-permute-start.11 = (bf16[512,384]{1,0:T(8,128)(2,1)}, bf16[512,384]{1,0:T(8,128)(2,1)}, u32[]{:S(2)}, u32[]{:S(2)}) collective-permute-start(bf16[512,384]{1,0:T(8,128)(2,1)} %get-tuple-element.104.rest_0_), channel_id=1, source_target_pairs={{0,1},{1,0},{2,3},{3,2},{4,5},{5,4},{6,7},{7,6},{8,9},{9,8},{10,11... | collective-permute-start | bytes 1179656 | tf_op jit(solution)/shard_map/ppermute | solution.py:433
  359.0 80.0 %collective-permute-start.12 = (bf16[512,384]{1,0:T(8,128)(2,1)}, bf16[512,384]{1,0:T(8,128)(2,1)}, u32[]{:S(2)}, u32[]{:S(2)}) collective-permute-start(bf16[512,384]{1,0:T(8,128)(2,1)} %get-tuple-element.104.rest_0_), channel_id=1, source_target_pairs={{0,2},{1,3},{2,0},{3,1},{4,6},{5,7},{6,4},{7,5},{8,10},{9,11},{10,... | collective-permute-start | bytes 1179656 | tf_op jit(solution)/shard_map/ppermute | solution.py:433
  374.6 64.3 %collective-permute-start.13 = (bf16[512,384]{1,0:T(8,128)(2,1)}, bf16[512,384]{1,0:T(8,128)(2,1)}, u32[]{:S(2)}, u32[]{:S(2)}) collective-permute-start(bf16[512,384]{1,0:T(8,128)(2,1)} %get-tuple-element.104.rest_0_), channel_id=1, source_target_pairs={{0,3},{1,2},{2,1},{3,0},{4,7},{5,6},{6,5},{7,4},{8,11},{9,10},{10,... | collective-permute-start | bytes 1179656 | tf_op jit(solution)/shard_map/ppermute | solution.py:433
  469.5 27.9 %all-to-all-start.9 = ((bf16[4,128,768]{2,1,0:T(8,128)(2,1)}), bf16[4,128,768]{2,1,0:T(8,128)(2,1)S(1)}, u32[]{:S(2)}, u32[]{:S(2)}) async-start(bf16[4,128,768]{2,1,0:T(8,128)(2,1)} %bitcast.25), calls=%async_computation.9 | async-start | bytes 1572864 | tf_op jit(solution)/shard_map/all_to_all | solution.py:438
  479.8 82.9 %all-reduce.10.cloned.1.call-start = ((), (), s32[]{:S(2)}) async-start(), calls=%async_computation.12 | async-start | bytes 7503872 | tf_op jit(solution)/shard_map/psum | solution.py:608
  515.5 20.1 %collective-permute-start.29 = (f32[2,768]{1,0:T(2,128)S(1)}, f32[2,768]{1,0:T(2,128)S(1)}, u32[]{:S(2)}, u32[]{:S(2)}) collective-permute-start(f32[2,768]{1,0:T(2,128)S(1)} %add.85), channel_id=1, source_target_pairs={{0,16},{4,20},{8,24},{12,28},{16,0},{20,4},{24,8},{28,12},{1,17},{... | collective-permute-start | bytes 18440 | tf_op jit(solution)/shard_map/ppermute | solution.py:628
  (64 other events, 1288.1 us)
Sparse Core Ops, SparseCore 0:
  485.4 77.2 all-reduce.9
